TPU v7x, 256 devices: a whole 4x4x8 slice. The times are simulated.
256 devices in a mesh: row: 16 (over z, y_lo), col: 16 (over y_hi, x, core).
Axes of the slice: x: 4, y: 4 (y_hi: 2, y_lo: 2; y = y_hi * 2 + y_lo), z: 8, core: 2. Of those that a mesh axis runs over, the one named last changes fastest.
Arguments:
- core_blocks: float32 [64, 2048, 128], P('row', 'col'), may hold values from -6 to 6
- block_coords: int32 [64, 32], replicated, may hold values from 0 to 9, as said below
- band_vectors: float32 [16, 16, 128], P('col'), may hold values from -6 to 6
- band_blocks: int32 [16, 16], P('col'), may hold values from 0 to 159, as said below
- spread: float32 [], replicated, may hold values from 12 to 24
Outputs:
- purified: float32 [64, 2048, 128], P('row', 'col')
Inputs may be any that keep to these rules, and one draw needn't show every extreme that they name: `block_coords`: the first entry of a slot is a local block row below 10, the second a local block column below 10; the 4 slots of one tile name distinct blocks. `band_blocks`: the 16 block rows of one band are distinct.
All inputs are finite; a program needn't handle non-finite values.
Results may differ from a plain program's by a relative error of at most 0.0003.
Values sent between devices are 32-bit elements; how exact they have to be, the bound alone decides.
A program may use at most 64 MiB of HBM per device.

v0:
```python
import jax
import jax.numpy as jnp
from jax import lax
from jax.sharding import PartitionSpec as P

NB = 160
highest = lax.Precision.HIGHEST


def shifted(block, axis, distance):
    devices = range(lax.axis_size(axis))
    route = [((i - distance) % len(devices), i) for i in devices]
    return lax.ppermute(block, axis, route)


def exchange_term(vectors, blocks, block_rows, block_cols):
    hit_row = (blocks[:, :, None] == block_rows[None, None, :]).astype(jnp.float32)
    hit_col = (blocks[:, :, None] == block_cols[None, None, :]).astype(jnp.float32)
    vec_row = jnp.einsum("bln,blx->bnx", hit_row, vectors, precision=highest)
    vec_col = jnp.einsum("bln,blx->bnx", hit_col, vectors, precision=highest)
    return -jnp.einsum("bnx,bny->nxy", vec_row, vec_col, precision=highest)


def tile_layout(layout, tile_row, tile_col):
    slots = layout.shape[1]
    start = (tile_row, jnp.int32(0), tile_col, jnp.int32(0))
    return lax.dynamic_slice(layout, start, (1, slots, 1, 2)).reshape(slots, 2)


def link_weights(targets, left_local, piece, right_local, tile_rows):
    row_target = targets[:, None, None, 0]
    col_target = targets[:, None, None, 1]
    row_left = left_local[None, :, None, 0]
    col_left = left_local[None, :, None, 1]
    row_right = right_local[None, None, :, 0]
    col_right = right_local[None, None, :, 1]
    keep = (row_left == row_target) & (col_left // tile_rows == piece)
    keep = keep & (col_left % tile_rows == row_right) & (col_right == col_target)
    return keep.astype(jnp.float32)


def accumulate(
    total, targets, left_blocks, left_local, piece, right_blocks, right_local, tile_rows
):
    weight = link_weights(targets, left_local, piece, right_local, tile_rows)
    pairs = jnp.einsum("axk,bky->axby", left_blocks, right_blocks, precision=highest)
    return total + jnp.einsum("tab,axby->txy", weight, pairs, precision=highest)


def advance(window):
    moved = shifted(window[0], "col", -1)
    return jnp.concatenate([window[1:], moved[None]], axis=0)


def align_right(right, this_col, ratio):
    row_count = lax.axis_size("row")
    amount = ratio * this_col % row_count
    for place in range((row_count - 1).bit_length()):
        moved = shifted(right, "row", -(1 << place))
        right = jnp.where(amount >> place & 1 == 1, moved, right)
    return right


def align_left(left, this_row, ratio):
    column_count = lax.axis_size("col")
    window = jnp.stack([left] * ratio)
    amount = this_row // ratio
    for place in range((column_count - 1).bit_length()):
        moved = shifted(window, "col", -(1 << place))
        window = jnp.where(amount >> place & 1 == 1, moved, window)
    return window


def shifted_product(left, right, layout, targets, this_row, this_col, tile_rows, ratio):
    row_count = lax.axis_size("row")
    window = align_left(left, this_row, ratio)

    def step_body(step, carry):
        total, window, right = carry
        source = (this_row + ratio * this_col + step) % row_count
        left_local = tile_layout(layout, this_row, source // ratio)
        right_local = tile_layout(layout, source, this_col)
        total = accumulate(
            total, targets, window[0], left_local, source % ratio, right, right_local, tile_rows
        )
        window = advance(window)
        right = shifted(right, "row", -1)
        return (total, window, right)

    total, window, right = lax.fori_loop(
        0, row_count, step_body, (jnp.zeros_like(left), window, right)
    )
    return (total, right)


def on_device(core_blocks, block_coords, band_vectors, band_blocks, spread):
    row_count = lax.axis_size("row")
    column_count = lax.axis_size("col")
    tile_rows = NB // row_count
    tile_columns = NB // column_count
    ratio = row_count // column_count
    slots = core_blocks.shape[0]
    this_row = lax.axis_index("row")
    this_col = lax.axis_index("col")
    layout = block_coords.reshape(row_count, slots, column_count, 2)
    targets = tile_layout(layout, this_row, this_col)
    vectors, blocks = (
        lax.all_gather(band_vectors, "col", axis=0, tiled=True),
        lax.all_gather(band_blocks, "col", axis=0, tiled=True),
    )
    block_rows = this_row * tile_rows + targets[:, 0]
    block_cols = this_col * tile_columns + targets[:, 1]
    exchange = exchange_term(vectors, blocks, block_rows, block_cols)
    fock = core_blocks + exchange
    scaled = fock / spread
    right = align_right(scaled, this_col, ratio)
    square, right = shifted_product(
        scaled, right, layout, targets, this_row, this_col, tile_rows, ratio
    )
    cube, right = shifted_product(
        square, right, layout, targets, this_row, this_col, tile_rows, ratio
    )
    return 1.5 * fock - 2.0 * spread * cube


def solution(mesh):
    placed = (P("row", "col", None), P(), P("col", None, None), P("col", None), P())
    return jax.shard_map(
        on_device, mesh=mesh, in_specs=placed, out_specs=P("row", "col", None), check_vma=False
    )
```

profile of v0, /device:TPU:6, one launch (start us, length us, event | category | flops | bytes accessed | tf_op | source)
XLA Modules:
  0.0 540.6 jit_solution(16270872847556958908)
XLA Ops:
  1.4 18.7 %all_gather.7 = f32[16,16,128]{2,1,0:T(8,128)S(1)} all-gather(f32[1,16,128]{2,1,0:T(8,128)S(1)} %copy-done.1), channel_id=1, replica_groups=mesh['row'=16,'col'=16] {'col'}, dimensions={0}, use_global_device_ids=true | all-gather | bytes 139264 | tf_op jit(solution)/shard_map/all_gather | solution.py:108
  20.8 21.4 %all-gather = s32[16,1,16]{2,1,0:T(1,128)S(1)} all-gather(s32[1,1,16]{2,1,0:T(1,128)S(1)} %bitcast.174), channel_id=1, replica_groups=mesh['row'=16,'col'=16] {'col'}, dimensions={0}, use_global_device_ids=true | all-gather | bytes 1088 | tf_op jit(solution)/shard_map/all_gather | solution.py:109
  44.1 6.9 %collective-permute-start.8 = (f32[4,128,128]{2,1,0:T(8,128)S(1)}, f32[4,128,128]{2,1,0:T(8,128)S(1)}, u32[]{:S(2)}, u32[]{:S(2)}) collective-permute-start(f32[4,128,128]{2,1,0:T(8,128)S(1)} %get-tuple-element.699), channel_id=1, source_target_pairs={{16,0},{32,16},{48,32},{64,48},{80,64},{96,80},{112,96},{128,112},... | collective-permute-start | bytes 786440 | tf_op jit(solution)/shard_map/ppermute | solution.py:13
  51.0 6.1 %collective-permute-done.8 = f32[4,128,128]{2,1,0:T(8,128)S(1)} collective-permute-done((f32[4,128,128]{2,1,0:T(8,128)S(1)}, f32[4,128,128]{2,1,0:T(8,128)S(1)}, u32[]{:S(2)}, u32[]{:S(2)}) %collective-permute-start.8) | collective-permute-done | bytes 262176 | tf_op jit(solution)/shard_map/ppermute | solution.py:13
  61.6 5.2 collective-permute-done.9
  72.6 5.4 collective-permute-done.10
  86.7 5.6 %collective-permute-done.11 = f32[4,128,128]{2,1,0:T(8,128)S(1)} collective-permute-done((f32[4,128,128]{2,1,0:T(8,128)S(1)}, f32[4,128,128]{2,1,0:T(8,128)S(1)}, u32[]{:S(2)}, u32[]{:S(2)}) %collective-permute-start.11) | collective-permute-done | bytes 262176 | tf_op jit(solution)/shard_map/ppermute | solution.py:13
  92.3 208.9 %while.42 = (s32[]{:T(128)}, f32[4,128,128]{2,0,1:T(4,128)S(1)}, f32[1,4,128,128]{3,2,1,0:T(8,128)S(1)}, f32[4,128,128]{2,1,0:T(8,128)S(1)}, s32[]{:T(128)}, /*i...) while((s32[]{:T(128)}, f32[4,128,128]{2,0,1:T(4,128)S(1)}, ...), condition=%wide.region_1.2_spmd.clone, body=%wide.region_0.1_spmd.clone.sunk | while | flops 415367424 | bytes 6292374 | solution.py:90
  92.5 8.7 %collective-permute-start.1 = (f32[4,128,128]{2,1,0:T(8,128)S(1)}, f32[4,128,128]{2,1,0:T(8,128)S(1)}, u32[]{:S(2)}, u32[]{:S(2)}) collective-permute-start(f32[4,128,128]{2,1,0:T(8,128)S(1)} %copy.54), channel_id=1, source_target_pairs={{16,0},{32,16},{48,32},{64,48},{80,64},{96,80},{112,96},{128,112},... | collective-permute-start | bytes 786440 | tf_op jit(solution)/shard_map/while/body/eval_jaxpr/ppermute | solution.py:13
  109.1 6.0 %collective-permute-start.1 = (f32[4,128,128]{2,1,0:T(8,128)S(1)}, f32[4,128,128]{2,1,0:T(8,128)S(1)}, u32[]{:S(2)}, u32[]{:S(2)}) collective-permute-start(f32[4,128,128]{2,1,0:T(8,128)S(1)} %copy.54), channel_id=1, source_target_pairs={{16,0},{32,16},{48,32},{64,48},{80,64},{96,80},{112,96},{128,112},... | collective-permute-start | bytes 786440 | tf_op jit(solution)/shard_map/while/body/eval_jaxpr/ppermute | solution.py:13
  118.1 5.9 %collective-permute-done.1 = f32[4,128,128]{2,1,0:T(8,128)S(1)} collective-permute-done((f32[4,128,128]{2,1,0:T(8,128)S(1)}, f32[4,128,128]{2,1,0:T(8,128)S(1)}, u32[]{:S(2)}, u32[]{:S(2)}) %collective-permute-start.1) | collective-permute-done | bytes 262176 | tf_op jit(solution)/shard_map/while/body/eval_jaxpr/ppermute | solution.py:13
  124.2 4.7 collective-permute-start.1
  132.0 5.0 collective-permute-done.1
  137.1 4.7 collective-permute-start.1
  148.5 4.7 collective-permute-start.1
  156.3 4.8 collective-permute-done.1
  161.3 4.7 collective-permute-start.1
  169.1 5.9 %collective-permute-done.1 = f32[4,128,128]{2,1,0:T(8,128)S(1)} collective-permute-done((f32[4,128,128]{2,1,0:T(8,128)S(1)}, f32[4,128,128]{2,1,0:T(8,128)S(1)}, u32[]{:S(2)}, u32[]{:S(2)}) %collective-permute-start.1) | collective-permute-done | bytes 262176 | tf_op jit(solution)/shard_map/while/body/eval_jaxpr/ppermute | solution.py:13
  175.1 4.7 collective-permute-start.1
  182.9 5.0 collective-permute-done.1
  188.0 4.7 collective-permute-start.1
  199.5 4.7 collective-permute-start.1
  207.3 4.8 collective-permute-done.1
  212.2 4.7 collective-permute-start.1
  220.0 5.9 %collective-permute-done.1 = f32[4,128,128]{2,1,0:T(8,128)S(1)} collective-permute-done((f32[4,128,128]{2,1,0:T(8,128)S(1)}, f32[4,128,128]{2,1,0:T(8,128)S(1)}, u32[]{:S(2)}, u32[]{:S(2)}) %collective-permute-start.1) | collective-permute-done | bytes 262176 | tf_op jit(solution)/shard_map/while/body/eval_jaxpr/ppermute | solution.py:13
  226.0 4.7 collective-permute-start.1
  233.8 5.0 collective-permute-done.1
  239.0 4.7 collective-permute-start.1
  250.4 4.7 collective-permute-start.1
  258.2 4.8 collective-permute-done.1
  263.1 4.7 collective-permute-start.1
  270.9 5.9 %collective-permute-done.1 = f32[4,128,128]{2,1,0:T(8,128)S(1)} collective-permute-done((f32[4,128,128]{2,1,0:T(8,128)S(1)}, f32[4,128,128]{2,1,0:T(8,128)S(1)}, u32[]{:S(2)}, u32[]{:S(2)}) %collective-permute-start.1) | collective-permute-done | bytes 262176 | tf_op jit(solution)/shard_map/while/body/eval_jaxpr/ppermute | solution.py:13
  277.0 4.7 collective-permute-start.1
  284.8 5.0 collective-permute-done.1
  289.9 4.7 collective-permute-start.1
  305.5 10.0 %collective-permute-done.13 = f32[1,4,128,128]{3,2,1,0:T(8,128)S(1)} collective-permute-done((f32[1,4,128,128]{3,2,1,0:T(8,128)S(1)}, f32[1,4,128,128]{3,2,1,0:T(8,128)S(1)}, u32[]{:S(2)}, u32[]{:S(2)}) %collective-permute-start.13) | collective-permute-done | bytes 262176 | tf_op jit(solution)/shard_map/ppermute | solution.py:13
  315.8 10.1 %collective-permute-done.14 = f32[1,4,128,128]{3,2,1,0:T(8,128)S(1)} collective-permute-done((f32[1,4,128,128]{3,2,1,0:T(8,128)S(1)}, f32[1,4,128,128]{3,2,1,0:T(8,128)S(1)}, u32[]{:S(2)}, u32[]{:S(2)}) %collective-permute-start.14) | collective-permute-done | bytes 262176 | tf_op jit(solution)/shard_map/ppermute | solution.py:13
  328.9 5.9 %collective-permute-done.15 = f32[1,4,128,128]{3,2,1,0:T(8,128)S(1)} collective-permute-done((f32[1,4,128,128]{3,2,1,0:T(8,128)S(1)}, f32[1,4,128,128]{3,2,1,0:T(8,128)S(1)}, u32[]{:S(2)}, u32[]{:S(2)}) %collective-permute-start.15) | collective-permute-done | bytes 262176 | tf_op jit(solution)/shard_map/ppermute | solution.py:13
  334.8 205.0 %while.43 = (s32[]{:T(128)}, f32[4,128,128]{2,0,1:T(4,128)S(1)}, f32[1,4,128,128]{3,2,1,0:T(8,128)S(1)}, f32[4,128,128]{2,1,0:T(8,128)S(1)}, s32[]{:T(128)}, /*i...) while((s32[]{:T(128)}, f32[4,128,128]{2,0,1:T(4,128)S(1)}, ...), condition=%wide.region_3.4_spmd.clone, body=%wide.region_2.3_spmd.clone.sunk | while | flops 415367424 | bytes 6292374 | solution.py:90
  335.0 4.8 collective-permute-start.3
  342.8 5.5 %collective-permute-done.3 = f32[4,128,128]{2,1,0:T(8,128)S(1)} collective-permute-done((f32[4,128,128]{2,1,0:T(8,128)S(1)}, f32[4,128,128]{2,1,0:T(8,128)S(1)}, u32[]{:S(2)}, u32[]{:S(2)}) %collective-permute-start.3) | collective-permute-done | bytes 262176 | tf_op jit(solution)/shard_map/while/body/eval_jaxpr/ppermute | solution.py:13
  348.5 4.9 collective-permute-start.3
  356.5 5.2 collective-permute-done.3
  361.8 4.7 collective-permute-start.3
  374.1 4.7 collective-permute-start.3
  381.9 5.2 collective-permute-done.3
  387.2 4.7 collective-permute-start.3
  395.0 5.7 %collective-permute-done.3 = f32[4,128,128]{2,1,0:T(8,128)S(1)} collective-permute-done((f32[4,128,128]{2,1,0:T(8,128)S(1)}, f32[4,128,128]{2,1,0:T(8,128)S(1)}, u32[]{:S(2)}, u32[]{:S(2)}) %collective-permute-start.3) | collective-permute-done | bytes 262176 | tf_op jit(solution)/shard_map/while/body/eval_jaxpr/ppermute | solution.py:13
  400.9 4.7 collective-permute-start.3
  413.0 4.7 collective-permute-start.3
  425.0 4.7 collective-permute-start.3
  432.8 5.2 collective-permute-done.3
  438.2 4.7 collective-permute-start.3
  446.0 5.7 %collective-permute-done.3 = f32[4,128,128]{2,1,0:T(8,128)S(1)} collective-permute-done((f32[4,128,128]{2,1,0:T(8,128)S(1)}, f32[4,128,128]{2,1,0:T(8,128)S(1)}, u32[]{:S(2)}, u32[]{:S(2)}) %collective-permute-start.3) | collective-permute-done | bytes 262176 | tf_op jit(solution)/shard_map/while/body/eval_jaxpr/ppermute | solution.py:13
  451.8 4.7 collective-permute-start.3
  464.0 4.7 collective-permute-start.3
  476.0 4.7 collective-permute-start.3
  483.8 5.2 collective-permute-done.3
  489.1 4.7 collective-permute-start.3
  496.9 5.7 %collective-permute-done.3 = f32[4,128,128]{2,1,0:T(8,128)S(1)} collective-permute-done((f32[4,128,128]{2,1,0:T(8,128)S(1)}, f32[4,128,128]{2,1,0:T(8,128)S(1)}, u32[]{:S(2)}, u32[]{:S(2)}) %collective-permute-start.3) | collective-permute-done | bytes 262176 | tf_op jit(solution)/shard_map/while/body/eval_jaxpr/ppermute | solution.py:13
  502.8 4.7 collective-permute-start.3
  514.9 4.7 collective-permute-start.3
  526.9 4.7 collective-permute-start.3
  534.7 5.2 collective-permute-done.3
  (507 shorter events, 178.9 us)
Async XLA Ops:
  44.1 13.0 %collective-permute-start.8 = (f32[4,128,128]{2,1,0:T(8,128)S(1)}, f32[4,128,128]{2,1,0:T(8,128)S(1)}, u32[]{:S(2)}, u32[]{:S(2)}) collective-permute-start(f32[4,128,128]{2,1,0:T(8,128)S(1)} %get-tuple-element.699), channel_id=1, source_target_pairs={{16,0},{32,16},{48,32},{64,48},{80,64},{96,80},{112,96},{128,112},... | collective-permute-start | bytes 786440 | tf_op jit(solution)/shard_map/ppermute | solution.py:13
  51.0 10.5 %collective-permute-start.4 = (f32[1,4,128,128]{3,2,1,0:T(8,128)S(1)}, f32[1,4,128,128]{3,2,1,0:T(8,128)S(1)}, u32[]{:S(2)}, u32[]{:S(2)}) collective-permute-start(f32[1,4,128,128]{3,2,1,0:T(8,128)S(1)} %bitcast.168), channel_id=1, source_target_pairs={{1,0},{2,1},{3,2},{4,3},{5,4},{6,5},{7,6},{8,7},{9,8},{10,9},{11,1... | collective-permute-start | bytes 786440 | tf_op jit(solution)/shard_map/ppermute | solution.py:13
  57.1 9.7 %collective-permute-start.9 = (f32[4,128,128]{2,1,0:T(8,128)S(1)}, f32[4,128,128]{2,1,0:T(8,128)S(1)}, u32[]{:S(2)}, u32[]{:S(2)}) collective-permute-start(f32[4,128,128]{2,1,0:T(8,128)S(1)} %broadcast_select_fusion), channel_id=1, source_target_pairs={{32,0},{48,16},{64,32},{80,48},{96,64},{112,80},{128,96},{144,112}... | collective-permute-start | bytes 786440 | tf_op jit(solution)/shard_map/ppermute | solution.py:13
  61.5 10.9 %collective-permute-start.5 = (f32[1,4,128,128]{3,2,1,0:T(8,128)S(1)}, f32[1,4,128,128]{3,2,1,0:T(8,128)S(1)}, u32[]{:S(2)}, u32[]{:S(2)}) collective-permute-start(f32[1,4,128,128]{3,2,1,0:T(8,128)S(1)} %broadcast_select_fusion.5), channel_id=1, source_target_pairs={{2,0},{3,1},{4,2},{5,3},{6,4},{7,5},{8,6},{9,7},{10,8},{11,9},{12,... | collective-permute-start | bytes 786440 | tf_op jit(solution)/shard_map/ppermute | solution.py:13
  66.8 11.1 %collective-permute-start.10 = (f32[4,128,128]{2,1,0:T(8,128)S(1)}, f32[4,128,128]{2,1,0:T(8,128)S(1)}, u32[]{:S(2)}, u32[]{:S(2)}) collective-permute-start(f32[4,128,128]{2,1,0:T(8,128)S(1)} %broadcast_select_fusion.1), channel_id=1, source_target_pairs={{64,0},{80,16},{96,32},{112,48},{128,64},{144,80},{160,96},{176,11... | collective-permute-start | bytes 786440 | tf_op jit(solution)/shard_map/ppermute | solution.py:13
  72.5 10.4 %collective-permute-start.6 = (f32[1,4,128,128]{3,2,1,0:T(8,128)S(1)}, f32[1,4,128,128]{3,2,1,0:T(8,128)S(1)}, u32[]{:S(2)}, u32[]{:S(2)}) collective-permute-start(f32[1,4,128,128]{3,2,1,0:T(8,128)S(1)} %broadcast_select_fusion.7), channel_id=1, source_target_pairs={{4,0},{5,1},{6,2},{7,3},{8,4},{9,5},{10,6},{11,7},{12,8},{13,9},{1... | collective-permute-start | bytes 786440 | tf_op jit(solution)/shard_map/ppermute | solution.py:13
  78.0 14.3 %collective-permute-start.11 = (f32[4,128,128]{2,1,0:T(8,128)S(1)}, f32[4,128,128]{2,1,0:T(8,128)S(1)}, u32[]{:S(2)}, u32[]{:S(2)}) collective-permute-start(f32[4,128,128]{2,1,0:T(8,128)S(1)} %broadcast_select_fusion.2), channel_id=1, source_target_pairs={{128,0},{144,16},{160,32},{176,48},{192,64},{208,80},{224,96},{240... | collective-permute-start | bytes 786440 | tf_op jit(solution)/shard_map/ppermute | solution.py:13
  82.8 9.5 %collective-permute-start.7 = (f32[1,4,128,128]{3,2,1,0:T(8,128)S(1)}, f32[1,4,128,128]{3,2,1,0:T(8,128)S(1)}, u32[]{:S(2)}, u32[]{:S(2)}) collective-permute-start(f32[1,4,128,128]{3,2,1,0:T(8,128)S(1)} %broadcast_select_fusion.9), channel_id=1, source_target_pairs={{8,0},{9,1},{10,2},{11,3},{12,4},{13,5},{14,6},{15,7},{0,8},{1,9},... | collective-permute-start | bytes 786440 | tf_op jit(solution)/shard_map/ppermute | solution.py:13
  92.4 11.9 %collective-permute-start = (f32[4,128,128]{2,1,0:T(8,128)S(1)}, f32[4,128,128]{2,1,0:T(8,128)S(1)}, u32[]{:S(2)}, u32[]{:S(2)}) collective-permute-start(f32[4,128,128]{2,1,0:T(8,128)S(1)} %bitcast.164), channel_id=1, source_target_pairs={{1,0},{2,1},{3,2},{4,3},{5,4},{6,5},{7,6},{8,7},{9,8},{10,9},{11,1... | collective-permute-start | bytes 786440 | tf_op jit(solution)/shard_map/while/body/eval_jaxpr/ppermute | solution.py:13
  92.5 16.4 %collective-permute-start.1 = (f32[4,128,128]{2,1,0:T(8,128)S(1)}, f32[4,128,128]{2,1,0:T(8,128)S(1)}, u32[]{:S(2)}, u32[]{:S(2)}) collective-permute-start(f32[4,128,128]{2,1,0:T(8,128)S(1)} %copy.54), channel_id=1, source_target_pairs={{16,0},{32,16},{48,32},{64,48},{80,64},{96,80},{112,96},{128,112},... | collective-permute-start | bytes 786440 | tf_op jit(solution)/shard_map/while/body/eval_jaxpr/ppermute | solution.py:13
  109.0 9.2 %collective-permute-start = (f32[4,128,128]{2,1,0:T(8,128)S(1)}, f32[4,128,128]{2,1,0:T(8,128)S(1)}, u32[]{:S(2)}, u32[]{:S(2)}) collective-permute-start(f32[4,128,128]{2,1,0:T(8,128)S(1)} %bitcast.164), channel_id=1, source_target_pairs={{1,0},{2,1},{3,2},{4,3},{5,4},{6,5},{7,6},{8,7},{9,8},{10,9},{11,1... | collective-permute-start | bytes 786440 | tf_op jit(solution)/shard_map/while/body/eval_jaxpr/ppermute | solution.py:13
  109.1 15.0 %collective-permute-start.1 = (f32[4,128,128]{2,1,0:T(8,128)S(1)}, f32[4,128,128]{2,1,0:T(8,128)S(1)}, u32[]{:S(2)}, u32[]{:S(2)}) collective-permute-start(f32[4,128,128]{2,1,0:T(8,128)S(1)} %copy.54), channel_id=1, source_target_pairs={{16,0},{32,16},{48,32},{64,48},{80,64},{96,80},{112,96},{128,112},... | collective-permute-start | bytes 786440 | tf_op jit(solution)/shard_map/while/body/eval_jaxpr/ppermute | solution.py:13
  124.2 12.8 %collective-permute-start.1 = (f32[4,128,128]{2,1,0:T(8,128)S(1)}, f32[4,128,128]{2,1,0:T(8,128)S(1)}, u32[]{:S(2)}, u32[]{:S(2)}) collective-permute-start(f32[4,128,128]{2,1,0:T(8,128)S(1)} %copy.54), channel_id=1, source_target_pairs={{16,0},{32,16},{48,32},{64,48},{80,64},{96,80},{112,96},{128,112},... | collective-permute-start | bytes 786440 | tf_op jit(solution)/shard_map/while/body/eval_jaxpr/ppermute | solution.py:13
  137.1 11.3 %collective-permute-start.1 = (f32[4,128,128]{2,1,0:T(8,128)S(1)}, f32[4,128,128]{2,1,0:T(8,128)S(1)}, u32[]{:S(2)}, u32[]{:S(2)}) collective-permute-start(f32[4,128,128]{2,1,0:T(8,128)S(1)} %copy.54), channel_id=1, source_target_pairs={{16,0},{32,16},{48,32},{64,48},{80,64},{96,80},{112,96},{128,112},... | collective-permute-start | bytes 786440 | tf_op jit(solution)/shard_map/while/body/eval_jaxpr/ppermute | solution.py:13
  148.4 7.9 %collective-permute-start = (f32[4,128,128]{2,1,0:T(8,128)S(1)}, f32[4,128,128]{2,1,0:T(8,128)S(1)}, u32[]{:S(2)}, u32[]{:S(2)}) collective-permute-start(f32[4,128,128]{2,1,0:T(8,128)S(1)} %bitcast.164), channel_id=1, source_target_pairs={{1,0},{2,1},{3,2},{4,3},{5,4},{6,5},{7,6},{8,7},{9,8},{10,9},{11,1... | collective-permute-start | bytes 786440 | tf_op jit(solution)/shard_map/while/body/eval_jaxpr/ppermute | solution.py:13
  148.5 12.6 %collective-permute-start.1 = (f32[4,128,128]{2,1,0:T(8,128)S(1)}, f32[4,128,128]{2,1,0:T(8,128)S(1)}, u32[]{:S(2)}, u32[]{:S(2)}) collective-permute-start(f32[4,128,128]{2,1,0:T(8,128)S(1)} %copy.54), channel_id=1, source_target_pairs={{16,0},{32,16},{48,32},{64,48},{80,64},{96,80},{112,96},{128,112},... | collective-permute-start | bytes 786440 | tf_op jit(solution)/shard_map/while/body/eval_jaxpr/ppermute | solution.py:13
  161.2 7.9 %collective-permute-start = (f32[4,128,128]{2,1,0:T(8,128)S(1)}, f32[4,128,128]{2,1,0:T(8,128)S(1)}, u32[]{:S(2)}, u32[]{:S(2)}) collective-permute-start(f32[4,128,128]{2,1,0:T(8,128)S(1)} %bitcast.164), channel_id=1, source_target_pairs={{1,0},{2,1},{3,2},{4,3},{5,4},{6,5},{7,6},{8,7},{9,8},{10,9},{11,1... | collective-permute-start | bytes 786440 | tf_op jit(solution)/shard_map/while/body/eval_jaxpr/ppermute | solution.py:13
  161.3 13.7 %collective-permute-start.1 = (f32[4,128,128]{2,1,0:T(8,128)S(1)}, f32[4,128,128]{2,1,0:T(8,128)S(1)}, u32[]{:S(2)}, u32[]{:S(2)}) collective-permute-start(f32[4,128,128]{2,1,0:T(8,128)S(1)} %copy.54), channel_id=1, source_target_pairs={{16,0},{32,16},{48,32},{64,48},{80,64},{96,80},{112,96},{128,112},... | collective-permute-start | bytes 786440 | tf_op jit(solution)/shard_map/while/body/eval_jaxpr/ppermute | solution.py:13
  175.0 7.9 %collective-permute-start = (f32[4,128,128]{2,1,0:T(8,128)S(1)}, f32[4,128,128]{2,1,0:T(8,128)S(1)}, u32[]{:S(2)}, u32[]{:S(2)}) collective-permute-start(f32[4,128,128]{2,1,0:T(8,128)S(1)} %bitcast.164), channel_id=1, source_target_pairs={{1,0},{2,1},{3,2},{4,3},{5,4},{6,5},{7,6},{8,7},{9,8},{10,9},{11,1... | collective-permute-start | bytes 786440 | tf_op jit(solution)/shard_map/while/body/eval_jaxpr/ppermute | solution.py:13
  175.1 12.8 %collective-permute-start.1 = (f32[4,128,128]{2,1,0:T(8,128)S(1)}, f32[4,128,128]{2,1,0:T(8,128)S(1)}, u32[]{:S(2)}, u32[]{:S(2)}) collective-permute-start(f32[4,128,128]{2,1,0:T(8,128)S(1)} %copy.54), channel_id=1, source_target_pairs={{16,0},{32,16},{48,32},{64,48},{80,64},{96,80},{112,96},{128,112},... | collective-permute-start | bytes 786440 | tf_op jit(solution)/shard_map/while/body/eval_jaxpr/ppermute | solution.py:13
  187.9 7.9 %collective-permute-start = (f32[4,128,128]{2,1,0:T(8,128)S(1)}, f32[4,128,128]{2,1,0:T(8,128)S(1)}, u32[]{:S(2)}, u32[]{:S(2)}) collective-permute-start(f32[4,128,128]{2,1,0:T(8,128)S(1)} %bitcast.164), channel_id=1, source_target_pairs={{1,0},{2,1},{3,2},{4,3},{5,4},{6,5},{7,6},{8,7},{9,8},{10,9},{11,1... | collective-permute-start | bytes 786440 | tf_op jit(solution)/shard_map/while/body/eval_jaxpr/ppermute | solution.py:13
  188.0 11.3 %collective-permute-start.1 = (f32[4,128,128]{2,1,0:T(8,128)S(1)}, f32[4,128,128]{2,1,0:T(8,128)S(1)}, u32[]{:S(2)}, u32[]{:S(2)}) collective-permute-start(f32[4,128,128]{2,1,0:T(8,128)S(1)} %copy.54), channel_id=1, source_target_pairs={{16,0},{32,16},{48,32},{64,48},{80,64},{96,80},{112,96},{128,112},... | collective-permute-start | bytes 786440 | tf_op jit(solution)/shard_map/while/body/eval_jaxpr/ppermute | solution.py:13
  199.4 7.9 %collective-permute-start = (f32[4,128,128]{2,1,0:T(8,128)S(1)}, f32[4,128,128]{2,1,0:T(8,128)S(1)}, u32[]{:S(2)}, u32[]{:S(2)}) collective-permute-start(f32[4,128,128]{2,1,0:T(8,128)S(1)} %bitcast.164), channel_id=1, source_target_pairs={{1,0},{2,1},{3,2},{4,3},{5,4},{6,5},{7,6},{8,7},{9,8},{10,9},{11,1... | collective-permute-start | bytes 786440 | tf_op jit(solution)/shard_map/while/body/eval_jaxpr/ppermute | solution.py:13
  199.5 12.6 %collective-permute-start.1 = (f32[4,128,128]{2,1,0:T(8,128)S(1)}, f32[4,128,128]{2,1,0:T(8,128)S(1)}, u32[]{:S(2)}, u32[]{:S(2)}) collective-permute-start(f32[4,128,128]{2,1,0:T(8,128)S(1)} %copy.54), channel_id=1, source_target_pairs={{16,0},{32,16},{48,32},{64,48},{80,64},{96,80},{112,96},{128,112},... | collective-permute-start | bytes 786440 | tf_op jit(solution)/shard_map/while/body/eval_jaxpr/ppermute | solution.py:13
  212.1 7.9 %collective-permute-start = (f32[4,128,128]{2,1,0:T(8,128)S(1)}, f32[4,128,128]{2,1,0:T(8,128)S(1)}, u32[]{:S(2)}, u32[]{:S(2)}) collective-permute-start(f32[4,128,128]{2,1,0:T(8,128)S(1)} %bitcast.164), channel_id=1, source_target_pairs={{1,0},{2,1},{3,2},{4,3},{5,4},{6,5},{7,6},{8,7},{9,8},{10,9},{11,1... | collective-permute-start | bytes 786440 | tf_op jit(solution)/shard_map/while/body/eval_jaxpr/ppermute | solution.py:13
  212.2 13.7 %collective-permute-start.1 = (f32[4,128,128]{2,1,0:T(8,128)S(1)}, f32[4,128,128]{2,1,0:T(8,128)S(1)}, u32[]{:S(2)}, u32[]{:S(2)}) collective-permute-start(f32[4,128,128]{2,1,0:T(8,128)S(1)} %copy.54), channel_id=1, source_target_pairs={{16,0},{32,16},{48,32},{64,48},{80,64},{96,80},{112,96},{128,112},... | collective-permute-start | bytes 786440 | tf_op jit(solution)/shard_map/while/body/eval_jaxpr/ppermute | solution.py:13
  225.9 7.9 %collective-permute-start = (f32[4,128,128]{2,1,0:T(8,128)S(1)}, f32[4,128,128]{2,1,0:T(8,128)S(1)}, u32[]{:S(2)}, u32[]{:S(2)}) collective-permute-start(f32[4,128,128]{2,1,0:T(8,128)S(1)} %bitcast.164), channel_id=1, source_target_pairs={{1,0},{2,1},{3,2},{4,3},{5,4},{6,5},{7,6},{8,7},{9,8},{10,9},{11,1... | collective-permute-start | bytes 786440 | tf_op jit(solution)/shard_map/while/body/eval_jaxpr/ppermute | solution.py:13
  226.0 12.8 %collective-permute-start.1 = (f32[4,128,128]{2,1,0:T(8,128)S(1)}, f32[4,128,128]{2,1,0:T(8,128)S(1)}, u32[]{:S(2)}, u32[]{:S(2)}) collective-permute-start(f32[4,128,128]{2,1,0:T(8,128)S(1)} %copy.54), channel_id=1, source_target_pairs={{16,0},{32,16},{48,32},{64,48},{80,64},{96,80},{112,96},{128,112},... | collective-permute-start | bytes 786440 | tf_op jit(solution)/shard_map/while/body/eval_jaxpr/ppermute | solution.py:13
  238.9 7.9 %collective-permute-start = (f32[4,128,128]{2,1,0:T(8,128)S(1)}, f32[4,128,128]{2,1,0:T(8,128)S(1)}, u32[]{:S(2)}, u32[]{:S(2)}) collective-permute-start(f32[4,128,128]{2,1,0:T(8,128)S(1)} %bitcast.164), channel_id=1, source_target_pairs={{1,0},{2,1},{3,2},{4,3},{5,4},{6,5},{7,6},{8,7},{9,8},{10,9},{11,1... | collective-permute-start | bytes 786440 | tf_op jit(solution)/shard_map/while/body/eval_jaxpr/ppermute | solution.py:13
  239.0 11.3 %collective-permute-start.1 = (f32[4,128,128]{2,1,0:T(8,128)S(1)}, f32[4,128,128]{2,1,0:T(8,128)S(1)}, u32[]{:S(2)}, u32[]{:S(2)}) collective-permute-start(f32[4,128,128]{2,1,0:T(8,128)S(1)} %copy.54), channel_id=1, source_target_pairs={{16,0},{32,16},{48,32},{64,48},{80,64},{96,80},{112,96},{128,112},... | collective-permute-start | bytes 786440 | tf_op jit(solution)/shard_map/while/body/eval_jaxpr/ppermute | solution.py:13
  250.4 12.6 %collective-permute-start.1 = (f32[4,128,128]{2,1,0:T(8,128)S(1)}, f32[4,128,128]{2,1,0:T(8,128)S(1)}, u32[]{:S(2)}, u32[]{:S(2)}) collective-permute-start(f32[4,128,128]{2,1,0:T(8,128)S(1)} %copy.54), channel_id=1, source_target_pairs={{16,0},{32,16},{48,32},{64,48},{80,64},{96,80},{112,96},{128,112},... | collective-permute-start | bytes 786440 | tf_op jit(solution)/shard_map/while/body/eval_jaxpr/ppermute | solution.py:13
  263.1 13.7 %collective-permute-start.1 = (f32[4,128,128]{2,1,0:T(8,128)S(1)}, f32[4,128,128]{2,1,0:T(8,128)S(1)}, u32[]{:S(2)}, u32[]{:S(2)}) collective-permute-start(f32[4,128,128]{2,1,0:T(8,128)S(1)} %copy.54), channel_id=1, source_target_pairs={{16,0},{32,16},{48,32},{64,48},{80,64},{96,80},{112,96},{128,112},... | collective-permute-start | bytes 786440 | tf_op jit(solution)/shard_map/while/body/eval_jaxpr/ppermute | solution.py:13
  277.0 12.8 %collective-permute-start.1 = (f32[4,128,128]{2,1,0:T(8,128)S(1)}, f32[4,128,128]{2,1,0:T(8,128)S(1)}, u32[]{:S(2)}, u32[]{:S(2)}) collective-permute-start(f32[4,128,128]{2,1,0:T(8,128)S(1)} %copy.54), channel_id=1, source_target_pairs={{16,0},{32,16},{48,32},{64,48},{80,64},{96,80},{112,96},{128,112},... | collective-permute-start | bytes 786440 | tf_op jit(solution)/shard_map/while/body/eval_jaxpr/ppermute | solution.py:13
  289.9 11.3 %collective-permute-start.1 = (f32[4,128,128]{2,1,0:T(8,128)S(1)}, f32[4,128,128]{2,1,0:T(8,128)S(1)}, u32[]{:S(2)}, u32[]{:S(2)}) collective-permute-start(f32[4,128,128]{2,1,0:T(8,128)S(1)} %copy.54), channel_id=1, source_target_pairs={{16,0},{32,16},{48,32},{64,48},{80,64},{96,80},{112,96},{128,112},... | collective-permute-start | bytes 786440 | tf_op jit(solution)/shard_map/while/body/eval_jaxpr/ppermute | solution.py:13
  305.4 10.1 %collective-permute-start.13 = (f32[1,4,128,128]{3,2,1,0:T(8,128)S(1)}, f32[1,4,128,128]{3,2,1,0:T(8,128)S(1)}, u32[]{:S(2)}, u32[]{:S(2)}) collective-permute-start(f32[1,4,128,128]{3,2,1,0:T(8,128)S(1)} %broadcast_select_fusion.4), channel_id=1, source_target_pairs={{2,0},{3,1},{4,2},{5,3},{6,4},{7,5},{8,6},{9,7},{10,8},{11,9},{12,... | collective-permute-start | bytes 786440 | tf_op jit(solution)/shard_map/ppermute | solution.py:13
  315.5 10.4 %collective-permute-start.14 = (f32[1,4,128,128]{3,2,1,0:T(8,128)S(1)}, f32[1,4,128,128]{3,2,1,0:T(8,128)S(1)}, u32[]{:S(2)}, u32[]{:S(2)}) collective-permute-start(f32[1,4,128,128]{3,2,1,0:T(8,128)S(1)} %broadcast_select_fusion.6), channel_id=1, source_target_pairs={{4,0},{5,1},{6,2},{7,3},{8,4},{9,5},{10,6},{11,7},{12,8},{13,9},{1... | collective-permute-start | bytes 786440 | tf_op jit(solution)/shard_map/ppermute | solution.py:13
  325.9 8.9 %collective-permute-start.15 = (f32[1,4,128,128]{3,2,1,0:T(8,128)S(1)}, f32[1,4,128,128]{3,2,1,0:T(8,128)S(1)}, u32[]{:S(2)}, u32[]{:S(2)}) collective-permute-start(f32[1,4,128,128]{3,2,1,0:T(8,128)S(1)} %broadcast_select_fusion.8), channel_id=1, source_target_pairs={{8,0},{9,1},{10,2},{11,3},{12,4},{13,5},{14,6},{15,7},{0,8},{1,9},... | collective-permute-start | bytes 786440 | tf_op jit(solution)/shard_map/ppermute | solution.py:13
  334.9 8.0 %collective-permute-start.2 = (f32[4,128,128]{2,1,0:T(8,128)S(1)}, f32[4,128,128]{2,1,0:T(8,128)S(1)}, u32[]{:S(2)}, u32[]{:S(2)}) collective-permute-start(f32[4,128,128]{2,1,0:T(8,128)S(1)} %bitcast.165), channel_id=1, source_target_pairs={{1,0},{2,1},{3,2},{4,3},{5,4},{6,5},{7,6},{8,7},{9,8},{10,9},{11,1... | collective-permute-start | bytes 786440 | tf_op jit(solution)/shard_map/while/body/eval_jaxpr/ppermute | solution.py:13
  335.0 13.4 %collective-permute-start.3 = (f32[4,128,128]{2,1,0:T(8,128)S(1)}, f32[4,128,128]{2,1,0:T(8,128)S(1)}, u32[]{:S(2)}, u32[]{:S(2)}) collective-permute-start(f32[4,128,128]{2,1,0:T(8,128)S(1)} %copy.66), channel_id=1, source_target_pairs={{16,0},{32,16},{48,32},{64,48},{80,64},{96,80},{112,96},{128,112},... | collective-permute-start | bytes 786440 | tf_op jit(solution)/shard_map/while/body/eval_jaxpr/ppermute | solution.py:13
  348.4 8.1 %collective-permute-start.2 = (f32[4,128,128]{2,1,0:T(8,128)S(1)}, f32[4,128,128]{2,1,0:T(8,128)S(1)}, u32[]{:S(2)}, u32[]{:S(2)}) collective-permute-start(f32[4,128,128]{2,1,0:T(8,128)S(1)} %bitcast.165), channel_id=1, source_target_pairs={{1,0},{2,1},{3,2},{4,3},{5,4},{6,5},{7,6},{8,7},{9,8},{10,9},{11,1... | collective-permute-start | bytes 786440 | tf_op jit(solution)/shard_map/while/body/eval_jaxpr/ppermute | solution.py:13
  348.5 13.1 %collective-permute-start.3 = (f32[4,128,128]{2,1,0:T(8,128)S(1)}, f32[4,128,128]{2,1,0:T(8,128)S(1)}, u32[]{:S(2)}, u32[]{:S(2)}) collective-permute-start(f32[4,128,128]{2,1,0:T(8,128)S(1)} %copy.66), channel_id=1, source_target_pairs={{16,0},{32,16},{48,32},{64,48},{80,64},{96,80},{112,96},{128,112},... | collective-permute-start | bytes 786440 | tf_op jit(solution)/shard_map/while/body/eval_jaxpr/ppermute | solution.py:13
  361.7 7.9 %collective-permute-start.2 = (f32[4,128,128]{2,1,0:T(8,128)S(1)}, f32[4,128,128]{2,1,0:T(8,128)S(1)}, u32[]{:S(2)}, u32[]{:S(2)}) collective-permute-start(f32[4,128,128]{2,1,0:T(8,128)S(1)} %bitcast.165), channel_id=1, source_target_pairs={{1,0},{2,1},{3,2},{4,3},{5,4},{6,5},{7,6},{8,7},{9,8},{10,9},{11,1... | collective-permute-start | bytes 786440 | tf_op jit(solution)/shard_map/while/body/eval_jaxpr/ppermute | solution.py:13
  361.8 12.1 %collective-permute-start.3 = (f32[4,128,128]{2,1,0:T(8,128)S(1)}, f32[4,128,128]{2,1,0:T(8,128)S(1)}, u32[]{:S(2)}, u32[]{:S(2)}) collective-permute-start(f32[4,128,128]{2,1,0:T(8,128)S(1)} %copy.66), channel_id=1, source_target_pairs={{16,0},{32,16},{48,32},{64,48},{80,64},{96,80},{112,96},{128,112},... | collective-permute-start | bytes 786440 | tf_op jit(solution)/shard_map/while/body/eval_jaxpr/ppermute | solution.py:13
  374.0 7.9 %collective-permute-start.2 = (f32[4,128,128]{2,1,0:T(8,128)S(1)}, f32[4,128,128]{2,1,0:T(8,128)S(1)}, u32[]{:S(2)}, u32[]{:S(2)}) collective-permute-start(f32[4,128,128]{2,1,0:T(8,128)S(1)} %bitcast.165), channel_id=1, source_target_pairs={{1,0},{2,1},{3,2},{4,3},{5,4},{6,5},{7,6},{8,7},{9,8},{10,9},{11,1... | collective-permute-start | bytes 786440 | tf_op jit(solution)/shard_map/while/body/eval_jaxpr/ppermute | solution.py:13
  374.1 13.0 %collective-permute-start.3 = (f32[4,128,128]{2,1,0:T(8,128)S(1)}, f32[4,128,128]{2,1,0:T(8,128)S(1)}, u32[]{:S(2)}, u32[]{:S(2)}) collective-permute-start(f32[4,128,128]{2,1,0:T(8,128)S(1)} %copy.66), channel_id=1, source_target_pairs={{16,0},{32,16},{48,32},{64,48},{80,64},{96,80},{112,96},{128,112},... | collective-permute-start | bytes 786440 | tf_op jit(solution)/shard_map/while/body/eval_jaxpr/ppermute | solution.py:13
  387.2 13.5 %collective-permute-start.3 = (f32[4,128,128]{2,1,0:T(8,128)S(1)}, f32[4,128,128]{2,1,0:T(8,128)S(1)}, u32[]{:S(2)}, u32[]{:S(2)}) collective-permute-start(f32[4,128,128]{2,1,0:T(8,128)S(1)} %copy.66), channel_id=1, source_target_pairs={{16,0},{32,16},{48,32},{64,48},{80,64},{96,80},{112,96},{128,112},... | collective-permute-start | bytes 786440 | tf_op jit(solution)/shard_map/while/body/eval_jaxpr/ppermute | solution.py:13
  400.8 7.9 %collective-permute-start.2 = (f32[4,128,128]{2,1,0:T(8,128)S(1)}, f32[4,128,128]{2,1,0:T(8,128)S(1)}, u32[]{:S(2)}, u32[]{:S(2)}) collective-permute-start(f32[4,128,128]{2,1,0:T(8,128)S(1)} %bitcast.165), channel_id=1, source_target_pairs={{1,0},{2,1},{3,2},{4,3},{5,4},{6,5},{7,6},{8,7},{9,8},{10,9},{11,1... | collective-permute-start | bytes 786440 | tf_op jit(solution)/shard_map/while/body/eval_jaxpr/ppermute | solution.py:13
  400.9 12.0 %collective-permute-start.3 = (f32[4,128,128]{2,1,0:T(8,128)S(1)}, f32[4,128,128]{2,1,0:T(8,128)S(1)}, u32[]{:S(2)}, u32[]{:S(2)}) collective-permute-start(f32[4,128,128]{2,1,0:T(8,128)S(1)} %copy.66), channel_id=1, source_target_pairs={{16,0},{32,16},{48,32},{64,48},{80,64},{96,80},{112,96},{128,112},... | collective-permute-start | bytes 786440 | tf_op jit(solution)/shard_map/while/body/eval_jaxpr/ppermute | solution.py:13
  412.9 7.9 %collective-permute-start.2 = (f32[4,128,128]{2,1,0:T(8,128)S(1)}, f32[4,128,128]{2,1,0:T(8,128)S(1)}, u32[]{:S(2)}, u32[]{:S(2)}) collective-permute-start(f32[4,128,128]{2,1,0:T(8,128)S(1)} %bitcast.165), channel_id=1, source_target_pairs={{1,0},{2,1},{3,2},{4,3},{5,4},{6,5},{7,6},{8,7},{9,8},{10,9},{11,1... | collective-permute-start | bytes 786440 | tf_op jit(solution)/shard_map/while/body/eval_jaxpr/ppermute | solution.py:13
  413.0 11.9 %collective-permute-start.3 = (f32[4,128,128]{2,1,0:T(8,128)S(1)}, f32[4,128,128]{2,1,0:T(8,128)S(1)}, u32[]{:S(2)}, u32[]{:S(2)}) collective-permute-start(f32[4,128,128]{2,1,0:T(8,128)S(1)} %copy.66), channel_id=1, source_target_pairs={{16,0},{32,16},{48,32},{64,48},{80,64},{96,80},{112,96},{128,112},... | collective-permute-start | bytes 786440 | tf_op jit(solution)/shard_map/while/body/eval_jaxpr/ppermute | solution.py:13
  424.9 7.9 %collective-permute-start.2 = (f32[4,128,128]{2,1,0:T(8,128)S(1)}, f32[4,128,128]{2,1,0:T(8,128)S(1)}, u32[]{:S(2)}, u32[]{:S(2)}) collective-permute-start(f32[4,128,128]{2,1,0:T(8,128)S(1)} %bitcast.165), channel_id=1, source_target_pairs={{1,0},{2,1},{3,2},{4,3},{5,4},{6,5},{7,6},{8,7},{9,8},{10,9},{11,1... | collective-permute-start | bytes 786440 | tf_op jit(solution)/shard_map/while/body/eval_jaxpr/ppermute | solution.py:13
  425.0 13.0 %collective-permute-start.3 = (f32[4,128,128]{2,1,0:T(8,128)S(1)}, f32[4,128,128]{2,1,0:T(8,128)S(1)}, u32[]{:S(2)}, u32[]{:S(2)}) collective-permute-start(f32[4,128,128]{2,1,0:T(8,128)S(1)} %copy.66), channel_id=1, source_target_pairs={{16,0},{32,16},{48,32},{64,48},{80,64},{96,80},{112,96},{128,112},... | collective-permute-start | bytes 786440 | tf_op jit(solution)/shard_map/while/body/eval_jaxpr/ppermute | solution.py:13
  438.0 7.9 %collective-permute-start.2 = (f32[4,128,128]{2,1,0:T(8,128)S(1)}, f32[4,128,128]{2,1,0:T(8,128)S(1)}, u32[]{:S(2)}, u32[]{:S(2)}) collective-permute-start(f32[4,128,128]{2,1,0:T(8,128)S(1)} %bitcast.165), channel_id=1, source_target_pairs={{1,0},{2,1},{3,2},{4,3},{5,4},{6,5},{7,6},{8,7},{9,8},{10,9},{11,1... | collective-permute-start | bytes 786440 | tf_op jit(solution)/shard_map/while/body/eval_jaxpr/ppermute | solution.py:13
  438.2 13.5 %collective-permute-start.3 = (f32[4,128,128]{2,1,0:T(8,128)S(1)}, f32[4,128,128]{2,1,0:T(8,128)S(1)}, u32[]{:S(2)}, u32[]{:S(2)}) collective-permute-start(f32[4,128,128]{2,1,0:T(8,128)S(1)} %copy.66), channel_id=1, source_target_pairs={{16,0},{32,16},{48,32},{64,48},{80,64},{96,80},{112,96},{128,112},... | collective-permute-start | bytes 786440 | tf_op jit(solution)/shard_map/while/body/eval_jaxpr/ppermute | solution.py:13
  451.7 7.9 %collective-permute-start.2 = (f32[4,128,128]{2,1,0:T(8,128)S(1)}, f32[4,128,128]{2,1,0:T(8,128)S(1)}, u32[]{:S(2)}, u32[]{:S(2)}) collective-permute-start(f32[4,128,128]{2,1,0:T(8,128)S(1)} %bitcast.165), channel_id=1, source_target_pairs={{1,0},{2,1},{3,2},{4,3},{5,4},{6,5},{7,6},{8,7},{9,8},{10,9},{11,1... | collective-permute-start | bytes 786440 | tf_op jit(solution)/shard_map/while/body/eval_jaxpr/ppermute | solution.py:13
  451.8 12.0 %collective-permute-start.3 = (f32[4,128,128]{2,1,0:T(8,128)S(1)}, f32[4,128,128]{2,1,0:T(8,128)S(1)}, u32[]{:S(2)}, u32[]{:S(2)}) collective-permute-start(f32[4,128,128]{2,1,0:T(8,128)S(1)} %copy.66), channel_id=1, source_target_pairs={{16,0},{32,16},{48,32},{64,48},{80,64},{96,80},{112,96},{128,112},... | collective-permute-start | bytes 786440 | tf_op jit(solution)/shard_map/while/body/eval_jaxpr/ppermute | solution.py:13
  464.0 11.9 %collective-permute-start.3 = (f32[4,128,128]{2,1,0:T(8,128)S(1)}, f32[4,128,128]{2,1,0:T(8,128)S(1)}, u32[]{:S(2)}, u32[]{:S(2)}) collective-permute-start(f32[4,128,128]{2,1,0:T(8,128)S(1)} %copy.66), channel_id=1, source_target_pairs={{16,0},{32,16},{48,32},{64,48},{80,64},{96,80},{112,96},{128,112},... | collective-permute-start | bytes 786440 | tf_op jit(solution)/shard_map/while/body/eval_jaxpr/ppermute | solution.py:13
  476.0 13.0 %collective-permute-start.3 = (f32[4,128,128]{2,1,0:T(8,128)S(1)}, f32[4,128,128]{2,1,0:T(8,128)S(1)}, u32[]{:S(2)}, u32[]{:S(2)}) collective-permute-start(f32[4,128,128]{2,1,0:T(8,128)S(1)} %copy.66), channel_id=1, source_target_pairs={{16,0},{32,16},{48,32},{64,48},{80,64},{96,80},{112,96},{128,112},... | collective-permute-start | bytes 786440 | tf_op jit(solution)/shard_map/while/body/eval_jaxpr/ppermute | solution.py:13
  489.0 7.9 %collective-permute-start.2 = (f32[4,128,128]{2,1,0:T(8,128)S(1)}, f32[4,128,128]{2,1,0:T(8,128)S(1)}, u32[]{:S(2)}, u32[]{:S(2)}) collective-permute-start(f32[4,128,128]{2,1,0:T(8,128)S(1)} %bitcast.165), channel_id=1, source_target_pairs={{1,0},{2,1},{3,2},{4,3},{5,4},{6,5},{7,6},{8,7},{9,8},{10,9},{11,1... | collective-permute-start | bytes 786440 | tf_op jit(solution)/shard_map/while/body/eval_jaxpr/ppermute | solution.py:13
  489.1 13.5 %collective-permute-start.3 = (f32[4,128,128]{2,1,0:T(8,128)S(1)}, f32[4,128,128]{2,1,0:T(8,128)S(1)}, u32[]{:S(2)}, u32[]{:S(2)}) collective-permute-start(f32[4,128,128]{2,1,0:T(8,128)S(1)} %copy.66), channel_id=1, source_target_pairs={{16,0},{32,16},{48,32},{64,48},{80,64},{96,80},{112,96},{128,112},... | collective-permute-start | bytes 786440 | tf_op jit(solution)/shard_map/while/body/eval_jaxpr/ppermute | solution.py:13
  502.8 12.0 %collective-permute-start.3 = (f32[4,128,128]{2,1,0:T(8,128)S(1)}, f32[4,128,128]{2,1,0:T(8,128)S(1)}, u32[]{:S(2)}, u32[]{:S(2)}) collective-permute-start(f32[4,128,128]{2,1,0:T(8,128)S(1)} %copy.66), channel_id=1, source_target_pairs={{16,0},{32,16},{48,32},{64,48},{80,64},{96,80},{112,96},{128,112},... | collective-permute-start | bytes 786440 | tf_op jit(solution)/shard_map/while/body/eval_jaxpr/ppermute | solution.py:13
  514.8 7.9 %collective-permute-start.2 = (f32[4,128,128]{2,1,0:T(8,128)S(1)}, f32[4,128,128]{2,1,0:T(8,128)S(1)}, u32[]{:S(2)}, u32[]{:S(2)}) collective-permute-start(f32[4,128,128]{2,1,0:T(8,128)S(1)} %bitcast.165), channel_id=1, source_target_pairs={{1,0},{2,1},{3,2},{4,3},{5,4},{6,5},{7,6},{8,7},{9,8},{10,9},{11,1... | collective-permute-start | bytes 786440 | tf_op jit(solution)/shard_map/while/body/eval_jaxpr/ppermute | solution.py:13
  514.9 11.9 %collective-permute-start.3 = (f32[4,128,128]{2,1,0:T(8,128)S(1)}, f32[4,128,128]{2,1,0:T(8,128)S(1)}, u32[]{:S(2)}, u32[]{:S(2)}) collective-permute-start(f32[4,128,128]{2,1,0:T(8,128)S(1)} %copy.66), channel_id=1, source_target_pairs={{16,0},{32,16},{48,32},{64,48},{80,64},{96,80},{112,96},{128,112},... | collective-permute-start | bytes 786440 | tf_op jit(solution)/shard_map/while/body/eval_jaxpr/ppermute | solution.py:13
  526.9 13.0 %collective-permute-start.3 = (f32[4,128,128]{2,1,0:T(8,128)S(1)}, f32[4,128,128]{2,1,0:T(8,128)S(1)}, u32[]{:S(2)}, u32[]{:S(2)}) collective-permute-start(f32[4,128,128]{2,1,0:T(8,128)S(1)} %copy.66), channel_id=1, source_target_pairs={{16,0},{32,16},{48,32},{64,48},{80,64},{96,80},{112,96},{128,112},... | collective-permute-start | bytes 786440 | tf_op jit(solution)/shard_map/while/body/eval_jaxpr/ppermute | solution.py:13
  (16 other events, 116.4 us)
where the time goes:
time: 541 us
  waiting for transfers between devices  214 us (40%)
  starting transfers between devices  181 us (33%)
  matrix products  89.2 us (16%)
  blocking collectives  40.2 us (7%)
  other arithmetic  9.19 us (2%)
    ppermute x76, waiting for transfers between devices, shifted(): return lax.ppermute(block, axis, route)  214 us
    ppermute x76, starting transfers between devices, shifted(): return lax.ppermute(block, axis, route)  181 us
    dot_general x32, matrix products, accumulate(): return total + jnp.einsum('tab,axby->txy', weight, pairs, precision=highest)  57 us
    dot_general x32, matrix products, accumulate(): jnp.einsum('axk,bky->axby', left_blocks, right_blocks, precision=highest)  31.1 us
    all_gather x1, blocking collectives, on_device(): lax.all_gather(band_blocks, 'col', axis=0, tiled=True)  21.4 us
    all_gather x1, blocking collectives, on_device(): lax.all_gather(band_vectors, 'col', axis=0, tiled=True)  18.7 us
  transfers between devices with their start and end apart: 76, of which 42 were waited for; matrix products, arithmetic and copies ran while one was open for 18% of the time, Pallas kernels for 0%

commit v1 on v0

--- a/solution.py
+++ b/solution.py
@@ -105,7 +105,9 @@
     layout = block_coords.reshape(row_count, slots, column_count, 2)
     targets = tile_layout(layout, this_row, this_col)
     vectors, blocks = (
-        lax.all_gather(band_vectors, "col", axis=0, tiled=True),
+        jnp.concatenate(
+            lax.all_to_all(jnp.stack([band_vectors] * lax.axis_size("col")), "col", 0, 0), axis=0
+        ),
         lax.all_gather(band_blocks, "col", axis=0, tiled=True),
     )
     block_rows = this_row * tile_rows + targets[:, 0]

time: 541 us -> 525 us (0.970)
  blocking collectives: 40.2 us -> 18.4 us
  starting transfers between devices: 181 us -> 194 us
  waiting for transfers between devices: 214 us -> 207 us
    all_gather x1 -> x0, blocking collectives: 18.7 us -> none  [on_device(): lax.all_gather(band_vectors, 'col', axis=0, tiled=True)]
    ppermute x76, waiting for transfers between devices: 214 us -> 207 us  [shifted(): return lax.ppermute(block, axis, route)]
    all_to_all x0 -> x1, starting transfers between devices: none -> 7.42 us  [on_device(): lax.all_to_all(jnp.stack([band_vectors] * lax.axis_size('col')), 'col', 0...]
  transfers between devices with their start and end apart: 76 -> 77, of which waited for: 42 -> 45; matrix products, arithmetic and copies ran while one was open for 18% -> 19% of each run, Pallas kernels for 0% -> 0%
where the time goes in v1:
time: 525 us; the launch traced here: 524 us
  waiting for transfers between devices  207 us (39%)
  starting transfers between devices  194 us (37%)
  matrix products  89.2 us (17%)
  blocking collectives  18.4 us (4%)
  other arithmetic  9.19 us (2%)
    ppermute x76, waiting for transfers between devices, shifted(): return lax.ppermute(block, axis, route)  207 us
    ppermute x76, starting transfers between devices, shifted(): return lax.ppermute(block, axis, route)  186 us
    dot_general x32, matrix products, accumulate(): return total + jnp.einsum('tab,axby->txy', weight, pairs, precision=highest)  57 us
    dot_general x32, matrix products, accumulate(): jnp.einsum('axk,bky->axby', left_blocks, right_blocks, precision=highest)  31.1 us
    all_gather x1, blocking collectives, on_device(): lax.all_gather(band_blocks, 'col', axis=0, tiled=True)  18.4 us
  transfers between devices with their start and end apart: 77, of which 45 were waited for; matrix products, arithmetic and copies ran while one was open for 19% of the time, Pallas kernels for 0%

profile of v1, /device:TPU:6, one launch (start us, length us, event | category | flops | bytes accessed | tf_op | source)
XLA Modules:
  0.0 524.3 jit_solution(10217276417954414676)
XLA Ops:
  1.4 7.4 %all-to-all-start = ((f32[16,1,16,128]{3,2,1,0:T(8,128)}), f32[16,1,16,128]{3,2,1,0:T(8,128)S(1)}, u32[]{:S(2)}, u32[]{:S(2)}) async-start(f32[16,1,16,128]{3,2,1,0:T(8,128)} %stack.6), calls=%async_computation | async-start | bytes 262144 | tf_op jit(solution)/shard_map/all_to_all | solution.py:109
  10.3 18.4 %all-gather = s32[16,1,16]{2,1,0:T(1,128)S(1)} all-gather(s32[1,1,16]{2,1,0:T(1,128)S(1)} %bitcast.179), channel_id=1, replica_groups=mesh['row'=16,'col'=16] {'col'}, dimensions={0}, use_global_device_ids=true | all-gather | bytes 1088 | tf_op jit(solution)/shard_map/all_gather | solution.py:111
  30.5 6.0 %collective-permute-start.8 = (f32[4,128,128]{2,1,0:T(8,128)S(1)}, f32[4,128,128]{2,1,0:T(8,128)S(1)}, u32[]{:S(2)}, u32[]{:S(2)}) collective-permute-start(f32[4,128,128]{2,1,0:T(8,128)S(1)} %get-tuple-element.717), channel_id=1, source_target_pairs={{16,0},{32,16},{48,32},{64,48},{80,64},{96,80},{112,96},{128,112},... | collective-permute-start | bytes 786440 | tf_op jit(solution)/shard_map/ppermute | solution.py:13
  53.2 4.5 collective-permute-done.5
  65.4 5.3 %collective-permute-done.6 = f32[1,4,128,128]{3,2,1,0:T(8,128)S(1)} collective-permute-done((f32[1,4,128,128]{3,2,1,0:T(8,128)S(1)}, f32[1,4,128,128]{3,2,1,0:T(8,128)S(1)}, u32[]{:S(2)}, u32[]{:S(2)}) %collective-permute-start.6) | collective-permute-done | bytes 262176 | tf_op jit(solution)/shard_map/ppermute | solution.py:13
  72.7 4.9 collective-permute-done.11
  80.3 206.9 %while.42 = (s32[]{:T(128)}, f32[4,128,128]{2,0,1:T(4,128)S(1)}, f32[1,4,128,128]{3,2,1,0:T(8,128)S(1)}, f32[4,128,128]{2,1,0:T(8,128)S(1)}, s32[]{:T(128)}, /*i...) while((s32[]{:T(128)}, f32[4,128,128]{2,0,1:T(4,128)S(1)}, ...), condition=%wide.region_1.2_spmd.clone, body=%wide.region_0.1_spmd.clone.sunk | while | flops 415367424 | bytes 6292374 | solution.py:90
  80.5 6.5 %collective-permute-start.1 = (f32[4,128,128]{2,1,0:T(8,128)S(1)}, f32[4,128,128]{2,1,0:T(8,128)S(1)}, u32[]{:S(2)}, u32[]{:S(2)}) collective-permute-start(f32[4,128,128]{2,1,0:T(8,128)S(1)} %copy.62), channel_id=1, source_target_pairs={{16,0},{32,16},{48,32},{64,48},{80,64},{96,80},{112,96},{128,112},... | collective-permute-start | bytes 786440 | tf_op jit(solution)/shard_map/while/body/eval_jaxpr/ppermute | solution.py:13
  94.2 4.8 collective-permute-start.1
  102.1 4.7 collective-permute-done.1
  107.0 5.9 %collective-permute-start.1 = (f32[4,128,128]{2,1,0:T(8,128)S(1)}, f32[4,128,128]{2,1,0:T(8,128)S(1)}, u32[]{:S(2)}, u32[]{:S(2)}) collective-permute-start(f32[4,128,128]{2,1,0:T(8,128)S(1)} %copy.62), channel_id=1, source_target_pairs={{16,0},{32,16},{48,32},{64,48},{80,64},{96,80},{112,96},{128,112},... | collective-permute-start | bytes 786440 | tf_op jit(solution)/shard_map/while/body/eval_jaxpr/ppermute | solution.py:13
  115.9 5.9 %collective-permute-done.1 = f32[4,128,128]{2,1,0:T(8,128)S(1)} collective-permute-done((f32[4,128,128]{2,1,0:T(8,128)S(1)}, f32[4,128,128]{2,1,0:T(8,128)S(1)}, u32[]{:S(2)}, u32[]{:S(2)}) %collective-permute-start.1) | collective-permute-done | bytes 262176 | tf_op jit(solution)/shard_map/while/body/eval_jaxpr/ppermute | solution.py:13
  122.0 4.7 collective-permute-start.1
  129.8 4.7 collective-permute-done.1
  134.6 4.7 collective-permute-start.1
  145.7 4.7 collective-permute-start.1
  153.5 5.4 %collective-permute-done.1 = f32[4,128,128]{2,1,0:T(8,128)S(1)} collective-permute-done((f32[4,128,128]{2,1,0:T(8,128)S(1)}, f32[4,128,128]{2,1,0:T(8,128)S(1)}, u32[]{:S(2)}, u32[]{:S(2)}) %collective-permute-start.1) | collective-permute-done | bytes 262176 | tf_op jit(solution)/shard_map/while/body/eval_jaxpr/ppermute | solution.py:13
  159.1 4.7 collective-permute-start.1
  166.9 5.9 %collective-permute-done.1 = f32[4,128,128]{2,1,0:T(8,128)S(1)} collective-permute-done((f32[4,128,128]{2,1,0:T(8,128)S(1)}, f32[4,128,128]{2,1,0:T(8,128)S(1)}, u32[]{:S(2)}, u32[]{:S(2)}) %collective-permute-start.1) | collective-permute-done | bytes 262176 | tf_op jit(solution)/shard_map/while/body/eval_jaxpr/ppermute | solution.py:13
  172.9 4.7 collective-permute-start.1
  180.7 4.7 collective-permute-done.1
  185.5 4.7 collective-permute-start.1
  197.0 4.7 collective-permute-start.1
  204.8 5.1 collective-permute-done.1
  210.0 4.7 collective-permute-start.1
  217.8 5.9 %collective-permute-done.1 = f32[4,128,128]{2,1,0:T(8,128)S(1)} collective-permute-done((f32[4,128,128]{2,1,0:T(8,128)S(1)}, f32[4,128,128]{2,1,0:T(8,128)S(1)}, u32[]{:S(2)}, u32[]{:S(2)}) %collective-permute-start.1) | collective-permute-done | bytes 262176 | tf_op jit(solution)/shard_map/while/body/eval_jaxpr/ppermute | solution.py:13
  223.8 4.7 collective-permute-start.1
  231.6 4.7 collective-permute-done.1
  236.5 4.7 collective-permute-start.1
  247.9 4.7 collective-permute-start.1
  255.7 5.1 collective-permute-done.1
  260.9 4.7 collective-permute-start.1
  268.7 5.9 %collective-permute-done.1 = f32[4,128,128]{2,1,0:T(8,128)S(1)} collective-permute-done((f32[4,128,128]{2,1,0:T(8,128)S(1)}, f32[4,128,128]{2,1,0:T(8,128)S(1)}, u32[]{:S(2)}, u32[]{:S(2)}) %collective-permute-start.1) | collective-permute-done | bytes 262176 | tf_op jit(solution)/shard_map/while/body/eval_jaxpr/ppermute | solution.py:13
  274.8 4.7 collective-permute-start.1
  282.6 4.7 collective-permute-done.1
  291.6 10.0 %collective-permute-done.13 = f32[1,4,128,128]{3,2,1,0:T(8,128)S(1)} collective-permute-done((f32[1,4,128,128]{3,2,1,0:T(8,128)S(1)}, f32[1,4,128,128]{3,2,1,0:T(8,128)S(1)}, u32[]{:S(2)}, u32[]{:S(2)}) %collective-permute-start.13) | collective-permute-done | bytes 262176 | tf_op jit(solution)/shard_map/ppermute | solution.py:13
  301.6 10.3 %collective-permute-done.14 = f32[1,4,128,128]{3,2,1,0:T(8,128)S(1)} collective-permute-done((f32[1,4,128,128]{3,2,1,0:T(8,128)S(1)}, f32[1,4,128,128]{3,2,1,0:T(8,128)S(1)}, u32[]{:S(2)}, u32[]{:S(2)}) %collective-permute-start.14) | collective-permute-done | bytes 262176 | tf_op jit(solution)/shard_map/ppermute | solution.py:13
  312.8 8.0 %collective-permute-done.15 = f32[1,4,128,128]{3,2,1,0:T(8,128)S(1)} collective-permute-done((f32[1,4,128,128]{3,2,1,0:T(8,128)S(1)}, f32[1,4,128,128]{3,2,1,0:T(8,128)S(1)}, u32[]{:S(2)}, u32[]{:S(2)}) %collective-permute-start.15) | collective-permute-done | bytes 262176 | tf_op jit(solution)/shard_map/ppermute | solution.py:13
  320.9 202.7 %while.43 = (s32[]{:T(128)}, f32[4,128,128]{2,0,1:T(4,128)S(1)}, f32[1,4,128,128]{3,2,1,0:T(8,128)S(1)}, f32[4,128,128]{2,1,0:T(8,128)S(1)}, s32[]{:T(128)}, /*i...) while((s32[]{:T(128)}, f32[4,128,128]{2,0,1:T(4,128)S(1)}, ...), condition=%wide.region_3.4_spmd.clone, body=%wide.region_2.3_spmd.clone.sunk | while | flops 415367424 | bytes 6292374 | solution.py:90
  321.0 4.8 collective-permute-start.3
  332.2 5.2 collective-permute-start.3
  343.7 5.1 collective-permute-start.3
  355.3 6.3 %collective-permute-start.3 = (f32[4,128,128]{2,1,0:T(8,128)S(1)}, f32[4,128,128]{2,1,0:T(8,128)S(1)}, u32[]{:S(2)}, u32[]{:S(2)}) collective-permute-start(f32[4,128,128]{2,1,0:T(8,128)S(1)} %copy.74), channel_id=1, source_target_pairs={{16,0},{32,16},{48,32},{64,48},{80,64},{96,80},{112,96},{128,112},... | collective-permute-start | bytes 786440 | tf_op jit(solution)/shard_map/while/body/eval_jaxpr/ppermute | solution.py:13
  364.7 4.8 collective-permute-done.3
  369.7 6.0 %collective-permute-start.3 = (f32[4,128,128]{2,1,0:T(8,128)S(1)}, f32[4,128,128]{2,1,0:T(8,128)S(1)}, u32[]{:S(2)}, u32[]{:S(2)}) collective-permute-start(f32[4,128,128]{2,1,0:T(8,128)S(1)} %copy.74), channel_id=1, source_target_pairs={{16,0},{32,16},{48,32},{64,48},{80,64},{96,80},{112,96},{128,112},... | collective-permute-start | bytes 786440 | tf_op jit(solution)/shard_map/while/body/eval_jaxpr/ppermute | solution.py:13
  378.8 5.6 %collective-permute-done.3 = f32[4,128,128]{2,1,0:T(8,128)S(1)} collective-permute-done((f32[4,128,128]{2,1,0:T(8,128)S(1)}, f32[4,128,128]{2,1,0:T(8,128)S(1)}, u32[]{:S(2)}, u32[]{:S(2)}) %collective-permute-start.3) | collective-permute-done | bytes 262176 | tf_op jit(solution)/shard_map/while/body/eval_jaxpr/ppermute | solution.py:13
  384.5 5.0 collective-permute-start.3
  392.6 5.3 %collective-permute-done.3 = f32[4,128,128]{2,1,0:T(8,128)S(1)} collective-permute-done((f32[4,128,128]{2,1,0:T(8,128)S(1)}, f32[4,128,128]{2,1,0:T(8,128)S(1)}, u32[]{:S(2)}, u32[]{:S(2)}) %collective-permute-start.3) | collective-permute-done | bytes 262176 | tf_op jit(solution)/shard_map/while/body/eval_jaxpr/ppermute | solution.py:13
  398.1 4.7 collective-permute-start.3
  409.8 4.7 collective-permute-start.3
  420.9 4.7 collective-permute-start.3
  428.7 5.5 %collective-permute-done.3 = f32[4,128,128]{2,1,0:T(8,128)S(1)} collective-permute-done((f32[4,128,128]{2,1,0:T(8,128)S(1)}, f32[4,128,128]{2,1,0:T(8,128)S(1)}, u32[]{:S(2)}, u32[]{:S(2)}) %collective-permute-start.3) | collective-permute-done | bytes 262176 | tf_op jit(solution)/shard_map/while/body/eval_jaxpr/ppermute | solution.py:13
  434.3 5.2 collective-permute-start.3
  442.5 5.9 %collective-permute-done.3 = f32[4,128,128]{2,1,0:T(8,128)S(1)} collective-permute-done((f32[4,128,128]{2,1,0:T(8,128)S(1)}, f32[4,128,128]{2,1,0:T(8,128)S(1)}, u32[]{:S(2)}, u32[]{:S(2)}) %collective-permute-start.3) | collective-permute-done | bytes 262176 | tf_op jit(solution)/shard_map/while/body/eval_jaxpr/ppermute | solution.py:13
  448.5 4.7 collective-permute-start.3
  456.3 4.9 collective-permute-done.3
  461.4 4.7 collective-permute-start.3
  472.6 4.7 collective-permute-start.3
  480.4 5.1 collective-permute-done.3
  485.6 4.7 collective-permute-start.3
  493.4 5.9 %collective-permute-done.3 = f32[4,128,128]{2,1,0:T(8,128)S(1)} collective-permute-done((f32[4,128,128]{2,1,0:T(8,128)S(1)}, f32[4,128,128]{2,1,0:T(8,128)S(1)}, u32[]{:S(2)}, u32[]{:S(2)}) %collective-permute-start.3) | collective-permute-done | bytes 262176 | tf_op jit(solution)/shard_map/while/body/eval_jaxpr/ppermute | solution.py:13
  499.5 4.7 collective-permute-start.3
  507.3 4.9 collective-permute-done.3
  512.3 4.7 collective-permute-start.3
  (507 shorter events, 177.3 us)
Async XLA Ops:
  1.4 28.0 %all-to-all-start = ((f32[16,1,16,128]{3,2,1,0:T(8,128)}), f32[16,1,16,128]{3,2,1,0:T(8,128)S(1)}, u32[]{:S(2)}, u32[]{:S(2)}) async-start(f32[16,1,16,128]{3,2,1,0:T(8,128)} %stack.6), calls=%async_computation | async-start | bytes 262144 | tf_op jit(solution)/shard_map/all_to_all | solution.py:109
  30.5 12.0 %collective-permute-start.8 = (f32[4,128,128]{2,1,0:T(8,128)S(1)}, f32[4,128,128]{2,1,0:T(8,128)S(1)}, u32[]{:S(2)}, u32[]{:S(2)}) collective-permute-start(f32[4,128,128]{2,1,0:T(8,128)S(1)} %get-tuple-element.717), channel_id=1, source_target_pairs={{16,0},{32,16},{48,32},{64,48},{80,64},{96,80},{112,96},{128,112},... | collective-permute-start | bytes 786440 | tf_op jit(solution)/shard_map/ppermute | solution.py:13
  36.6 8.5 %collective-permute-start.4 = (f32[1,4,128,128]{3,2,1,0:T(8,128)S(1)}, f32[1,4,128,128]{3,2,1,0:T(8,128)S(1)}, u32[]{:S(2)}, u32[]{:S(2)}) collective-permute-start(f32[1,4,128,128]{3,2,1,0:T(8,128)S(1)} %bitcast.172), channel_id=1, source_target_pairs={{1,0},{2,1},{3,2},{4,3},{5,4},{6,5},{7,6},{8,7},{9,8},{10,9},{11,1... | collective-permute-start | bytes 786440 | tf_op jit(solution)/shard_map/ppermute | solution.py:13
  45.1 12.6 %collective-permute-start.5 = (f32[1,4,128,128]{3,2,1,0:T(8,128)S(1)}, f32[1,4,128,128]{3,2,1,0:T(8,128)S(1)}, u32[]{:S(2)}, u32[]{:S(2)}) collective-permute-start(f32[1,4,128,128]{3,2,1,0:T(8,128)S(1)} %broadcast_select_fusion.5), channel_id=1, source_target_pairs={{2,0},{3,1},{4,2},{5,3},{6,4},{7,5},{8,6},{9,7},{10,8},{11,9},{12,... | collective-permute-start | bytes 786440 | tf_op jit(solution)/shard_map/ppermute | solution.py:13
  50.3 10.7 %collective-permute-start.10 = (f32[4,128,128]{2,1,0:T(8,128)S(1)}, f32[4,128,128]{2,1,0:T(8,128)S(1)}, u32[]{:S(2)}, u32[]{:S(2)}) collective-permute-start(f32[4,128,128]{2,1,0:T(8,128)S(1)} %broadcast_select_fusion.1), channel_id=1, source_target_pairs={{64,0},{80,16},{96,32},{112,48},{128,64},{144,80},{160,96},{176,11... | collective-permute-start | bytes 786440 | tf_op jit(solution)/shard_map/ppermute | solution.py:13
  57.7 12.9 %collective-permute-start.6 = (f32[1,4,128,128]{3,2,1,0:T(8,128)S(1)}, f32[1,4,128,128]{3,2,1,0:T(8,128)S(1)}, u32[]{:S(2)}, u32[]{:S(2)}) collective-permute-start(f32[1,4,128,128]{3,2,1,0:T(8,128)S(1)} %broadcast_select_fusion.7), channel_id=1, source_target_pairs={{4,0},{5,1},{6,2},{7,3},{8,4},{9,5},{10,6},{11,7},{12,8},{13,9},{1... | collective-permute-start | bytes 786440 | tf_op jit(solution)/shard_map/ppermute | solution.py:13
  61.0 16.6 %collective-permute-start.11 = (f32[4,128,128]{2,1,0:T(8,128)S(1)}, f32[4,128,128]{2,1,0:T(8,128)S(1)}, u32[]{:S(2)}, u32[]{:S(2)}) collective-permute-start(f32[4,128,128]{2,1,0:T(8,128)S(1)} %broadcast_select_fusion.2), channel_id=1, source_target_pairs={{128,0},{144,16},{160,32},{176,48},{192,64},{208,80},{224,96},{240... | collective-permute-start | bytes 786440 | tf_op jit(solution)/shard_map/ppermute | solution.py:13
  70.7 9.7 %collective-permute-start.7 = (f32[1,4,128,128]{3,2,1,0:T(8,128)S(1)}, f32[1,4,128,128]{3,2,1,0:T(8,128)S(1)}, u32[]{:S(2)}, u32[]{:S(2)}) collective-permute-start(f32[1,4,128,128]{3,2,1,0:T(8,128)S(1)} %broadcast_select_fusion.9), channel_id=1, source_target_pairs={{8,0},{9,1},{10,2},{11,3},{12,4},{13,5},{14,6},{15,7},{0,8},{1,9},... | collective-permute-start | bytes 786440 | tf_op jit(solution)/shard_map/ppermute | solution.py:13
  80.4 9.7 %collective-permute-start = (f32[4,128,128]{2,1,0:T(8,128)S(1)}, f32[4,128,128]{2,1,0:T(8,128)S(1)}, u32[]{:S(2)}, u32[]{:S(2)}) collective-permute-start(f32[4,128,128]{2,1,0:T(8,128)S(1)} %bitcast.168), channel_id=1, source_target_pairs={{1,0},{2,1},{3,2},{4,3},{5,4},{6,5},{7,6},{8,7},{9,8},{10,9},{11,1... | collective-permute-start | bytes 786440 | tf_op jit(solution)/shard_map/while/body/eval_jaxpr/ppermute | solution.py:13
  80.5 11.6 %collective-permute-start.1 = (f32[4,128,128]{2,1,0:T(8,128)S(1)}, f32[4,128,128]{2,1,0:T(8,128)S(1)}, u32[]{:S(2)}, u32[]{:S(2)}) collective-permute-start(f32[4,128,128]{2,1,0:T(8,128)S(1)} %copy.62), channel_id=1, source_target_pairs={{16,0},{32,16},{48,32},{64,48},{80,64},{96,80},{112,96},{128,112},... | collective-permute-start | bytes 786440 | tf_op jit(solution)/shard_map/while/body/eval_jaxpr/ppermute | solution.py:13
  92.1 10.0 %collective-permute-start = (f32[4,128,128]{2,1,0:T(8,128)S(1)}, f32[4,128,128]{2,1,0:T(8,128)S(1)}, u32[]{:S(2)}, u32[]{:S(2)}) collective-permute-start(f32[4,128,128]{2,1,0:T(8,128)S(1)} %bitcast.168), channel_id=1, source_target_pairs={{1,0},{2,1},{3,2},{4,3},{5,4},{6,5},{7,6},{8,7},{9,8},{10,9},{11,1... | collective-permute-start | bytes 786440 | tf_op jit(solution)/shard_map/while/body/eval_jaxpr/ppermute | solution.py:13
  94.2 12.6 %collective-permute-start.1 = (f32[4,128,128]{2,1,0:T(8,128)S(1)}, f32[4,128,128]{2,1,0:T(8,128)S(1)}, u32[]{:S(2)}, u32[]{:S(2)}) collective-permute-start(f32[4,128,128]{2,1,0:T(8,128)S(1)} %copy.62), channel_id=1, source_target_pairs={{16,0},{32,16},{48,32},{64,48},{80,64},{96,80},{112,96},{128,112},... | collective-permute-start | bytes 786440 | tf_op jit(solution)/shard_map/while/body/eval_jaxpr/ppermute | solution.py:13
  106.8 9.1 %collective-permute-start = (f32[4,128,128]{2,1,0:T(8,128)S(1)}, f32[4,128,128]{2,1,0:T(8,128)S(1)}, u32[]{:S(2)}, u32[]{:S(2)}) collective-permute-start(f32[4,128,128]{2,1,0:T(8,128)S(1)} %bitcast.168), channel_id=1, source_target_pairs={{1,0},{2,1},{3,2},{4,3},{5,4},{6,5},{7,6},{8,7},{9,8},{10,9},{11,1... | collective-permute-start | bytes 786440 | tf_op jit(solution)/shard_map/while/body/eval_jaxpr/ppermute | solution.py:13
  107.0 14.9 %collective-permute-start.1 = (f32[4,128,128]{2,1,0:T(8,128)S(1)}, f32[4,128,128]{2,1,0:T(8,128)S(1)}, u32[]{:S(2)}, u32[]{:S(2)}) collective-permute-start(f32[4,128,128]{2,1,0:T(8,128)S(1)} %copy.62), channel_id=1, source_target_pairs={{16,0},{32,16},{48,32},{64,48},{80,64},{96,80},{112,96},{128,112},... | collective-permute-start | bytes 786440 | tf_op jit(solution)/shard_map/while/body/eval_jaxpr/ppermute | solution.py:13
  122.0 12.5 %collective-permute-start.1 = (f32[4,128,128]{2,1,0:T(8,128)S(1)}, f32[4,128,128]{2,1,0:T(8,128)S(1)}, u32[]{:S(2)}, u32[]{:S(2)}) collective-permute-start(f32[4,128,128]{2,1,0:T(8,128)S(1)} %copy.62), channel_id=1, source_target_pairs={{16,0},{32,16},{48,32},{64,48},{80,64},{96,80},{112,96},{128,112},... | collective-permute-start | bytes 786440 | tf_op jit(solution)/shard_map/while/body/eval_jaxpr/ppermute | solution.py:13
  134.5 7.9 %collective-permute-start = (f32[4,128,128]{2,1,0:T(8,128)S(1)}, f32[4,128,128]{2,1,0:T(8,128)S(1)}, u32[]{:S(2)}, u32[]{:S(2)}) collective-permute-start(f32[4,128,128]{2,1,0:T(8,128)S(1)} %bitcast.168), channel_id=1, source_target_pairs={{1,0},{2,1},{3,2},{4,3},{5,4},{6,5},{7,6},{8,7},{9,8},{10,9},{11,1... | collective-permute-start | bytes 786440 | tf_op jit(solution)/shard_map/while/body/eval_jaxpr/ppermute | solution.py:13
  134.6 11.0 %collective-permute-start.1 = (f32[4,128,128]{2,1,0:T(8,128)S(1)}, f32[4,128,128]{2,1,0:T(8,128)S(1)}, u32[]{:S(2)}, u32[]{:S(2)}) collective-permute-start(f32[4,128,128]{2,1,0:T(8,128)S(1)} %copy.62), channel_id=1, source_target_pairs={{16,0},{32,16},{48,32},{64,48},{80,64},{96,80},{112,96},{128,112},... | collective-permute-start | bytes 786440 | tf_op jit(solution)/shard_map/while/body/eval_jaxpr/ppermute | solution.py:13
  145.7 13.2 %collective-permute-start.1 = (f32[4,128,128]{2,1,0:T(8,128)S(1)}, f32[4,128,128]{2,1,0:T(8,128)S(1)}, u32[]{:S(2)}, u32[]{:S(2)}) collective-permute-start(f32[4,128,128]{2,1,0:T(8,128)S(1)} %copy.62), channel_id=1, source_target_pairs={{16,0},{32,16},{48,32},{64,48},{80,64},{96,80},{112,96},{128,112},... | collective-permute-start | bytes 786440 | tf_op jit(solution)/shard_map/while/body/eval_jaxpr/ppermute | solution.py:13
  159.1 13.7 %collective-permute-start.1 = (f32[4,128,128]{2,1,0:T(8,128)S(1)}, f32[4,128,128]{2,1,0:T(8,128)S(1)}, u32[]{:S(2)}, u32[]{:S(2)}) collective-permute-start(f32[4,128,128]{2,1,0:T(8,128)S(1)} %copy.62), channel_id=1, source_target_pairs={{16,0},{32,16},{48,32},{64,48},{80,64},{96,80},{112,96},{128,112},... | collective-permute-start | bytes 786440 | tf_op jit(solution)/shard_map/while/body/eval_jaxpr/ppermute | solution.py:13
  172.9 12.5 %collective-permute-start.1 = (f32[4,128,128]{2,1,0:T(8,128)S(1)}, f32[4,128,128]{2,1,0:T(8,128)S(1)}, u32[]{:S(2)}, u32[]{:S(2)}) collective-permute-start(f32[4,128,128]{2,1,0:T(8,128)S(1)} %copy.62), channel_id=1, source_target_pairs={{16,0},{32,16},{48,32},{64,48},{80,64},{96,80},{112,96},{128,112},... | collective-permute-start | bytes 786440 | tf_op jit(solution)/shard_map/while/body/eval_jaxpr/ppermute | solution.py:13
  185.4 7.9 %collective-permute-start = (f32[4,128,128]{2,1,0:T(8,128)S(1)}, f32[4,128,128]{2,1,0:T(8,128)S(1)}, u32[]{:S(2)}, u32[]{:S(2)}) collective-permute-start(f32[4,128,128]{2,1,0:T(8,128)S(1)} %bitcast.168), channel_id=1, source_target_pairs={{1,0},{2,1},{3,2},{4,3},{5,4},{6,5},{7,6},{8,7},{9,8},{10,9},{11,1... | collective-permute-start | bytes 786440 | tf_op jit(solution)/shard_map/while/body/eval_jaxpr/ppermute | solution.py:13
  185.5 11.3 %collective-permute-start.1 = (f32[4,128,128]{2,1,0:T(8,128)S(1)}, f32[4,128,128]{2,1,0:T(8,128)S(1)}, u32[]{:S(2)}, u32[]{:S(2)}) collective-permute-start(f32[4,128,128]{2,1,0:T(8,128)S(1)} %copy.62), channel_id=1, source_target_pairs={{16,0},{32,16},{48,32},{64,48},{80,64},{96,80},{112,96},{128,112},... | collective-permute-start | bytes 786440 | tf_op jit(solution)/shard_map/while/body/eval_jaxpr/ppermute | solution.py:13
  197.0 12.9 %collective-permute-start.1 = (f32[4,128,128]{2,1,0:T(8,128)S(1)}, f32[4,128,128]{2,1,0:T(8,128)S(1)}, u32[]{:S(2)}, u32[]{:S(2)}) collective-permute-start(f32[4,128,128]{2,1,0:T(8,128)S(1)} %copy.62), channel_id=1, source_target_pairs={{16,0},{32,16},{48,32},{64,48},{80,64},{96,80},{112,96},{128,112},... | collective-permute-start | bytes 786440 | tf_op jit(solution)/shard_map/while/body/eval_jaxpr/ppermute | solution.py:13
  209.9 7.9 %collective-permute-start = (f32[4,128,128]{2,1,0:T(8,128)S(1)}, f32[4,128,128]{2,1,0:T(8,128)S(1)}, u32[]{:S(2)}, u32[]{:S(2)}) collective-permute-start(f32[4,128,128]{2,1,0:T(8,128)S(1)} %bitcast.168), channel_id=1, source_target_pairs={{1,0},{2,1},{3,2},{4,3},{5,4},{6,5},{7,6},{8,7},{9,8},{10,9},{11,1... | collective-permute-start | bytes 786440 | tf_op jit(solution)/shard_map/while/body/eval_jaxpr/ppermute | solution.py:13
  210.0 13.7 %collective-permute-start.1 = (f32[4,128,128]{2,1,0:T(8,128)S(1)}, f32[4,128,128]{2,1,0:T(8,128)S(1)}, u32[]{:S(2)}, u32[]{:S(2)}) collective-permute-start(f32[4,128,128]{2,1,0:T(8,128)S(1)} %copy.62), channel_id=1, source_target_pairs={{16,0},{32,16},{48,32},{64,48},{80,64},{96,80},{112,96},{128,112},... | collective-permute-start | bytes 786440 | tf_op jit(solution)/shard_map/while/body/eval_jaxpr/ppermute | solution.py:13
  223.7 7.9 %collective-permute-start = (f32[4,128,128]{2,1,0:T(8,128)S(1)}, f32[4,128,128]{2,1,0:T(8,128)S(1)}, u32[]{:S(2)}, u32[]{:S(2)}) collective-permute-start(f32[4,128,128]{2,1,0:T(8,128)S(1)} %bitcast.168), channel_id=1, source_target_pairs={{1,0},{2,1},{3,2},{4,3},{5,4},{6,5},{7,6},{8,7},{9,8},{10,9},{11,1... | collective-permute-start | bytes 786440 | tf_op jit(solution)/shard_map/while/body/eval_jaxpr/ppermute | solution.py:13
  223.8 12.5 %collective-permute-start.1 = (f32[4,128,128]{2,1,0:T(8,128)S(1)}, f32[4,128,128]{2,1,0:T(8,128)S(1)}, u32[]{:S(2)}, u32[]{:S(2)}) collective-permute-start(f32[4,128,128]{2,1,0:T(8,128)S(1)} %copy.62), channel_id=1, source_target_pairs={{16,0},{32,16},{48,32},{64,48},{80,64},{96,80},{112,96},{128,112},... | collective-permute-start | bytes 786440 | tf_op jit(solution)/shard_map/while/body/eval_jaxpr/ppermute | solution.py:13
  236.5 11.3 %collective-permute-start.1 = (f32[4,128,128]{2,1,0:T(8,128)S(1)}, f32[4,128,128]{2,1,0:T(8,128)S(1)}, u32[]{:S(2)}, u32[]{:S(2)}) collective-permute-start(f32[4,128,128]{2,1,0:T(8,128)S(1)} %copy.62), channel_id=1, source_target_pairs={{16,0},{32,16},{48,32},{64,48},{80,64},{96,80},{112,96},{128,112},... | collective-permute-start | bytes 786440 | tf_op jit(solution)/shard_map/while/body/eval_jaxpr/ppermute | solution.py:13
  247.8 7.9 %collective-permute-start = (f32[4,128,128]{2,1,0:T(8,128)S(1)}, f32[4,128,128]{2,1,0:T(8,128)S(1)}, u32[]{:S(2)}, u32[]{:S(2)}) collective-permute-start(f32[4,128,128]{2,1,0:T(8,128)S(1)} %bitcast.168), channel_id=1, source_target_pairs={{1,0},{2,1},{3,2},{4,3},{5,4},{6,5},{7,6},{8,7},{9,8},{10,9},{11,1... | collective-permute-start | bytes 786440 | tf_op jit(solution)/shard_map/while/body/eval_jaxpr/ppermute | solution.py:13
  247.9 12.9 %collective-permute-start.1 = (f32[4,128,128]{2,1,0:T(8,128)S(1)}, f32[4,128,128]{2,1,0:T(8,128)S(1)}, u32[]{:S(2)}, u32[]{:S(2)}) collective-permute-start(f32[4,128,128]{2,1,0:T(8,128)S(1)} %copy.62), channel_id=1, source_target_pairs={{16,0},{32,16},{48,32},{64,48},{80,64},{96,80},{112,96},{128,112},... | collective-permute-start | bytes 786440 | tf_op jit(solution)/shard_map/while/body/eval_jaxpr/ppermute | solution.py:13
  260.8 7.9 %collective-permute-start = (f32[4,128,128]{2,1,0:T(8,128)S(1)}, f32[4,128,128]{2,1,0:T(8,128)S(1)}, u32[]{:S(2)}, u32[]{:S(2)}) collective-permute-start(f32[4,128,128]{2,1,0:T(8,128)S(1)} %bitcast.168), channel_id=1, source_target_pairs={{1,0},{2,1},{3,2},{4,3},{5,4},{6,5},{7,6},{8,7},{9,8},{10,9},{11,1... | collective-permute-start | bytes 786440 | tf_op jit(solution)/shard_map/while/body/eval_jaxpr/ppermute | solution.py:13
  260.9 13.7 %collective-permute-start.1 = (f32[4,128,128]{2,1,0:T(8,128)S(1)}, f32[4,128,128]{2,1,0:T(8,128)S(1)}, u32[]{:S(2)}, u32[]{:S(2)}) collective-permute-start(f32[4,128,128]{2,1,0:T(8,128)S(1)} %copy.62), channel_id=1, source_target_pairs={{16,0},{32,16},{48,32},{64,48},{80,64},{96,80},{112,96},{128,112},... | collective-permute-start | bytes 786440 | tf_op jit(solution)/shard_map/while/body/eval_jaxpr/ppermute | solution.py:13
  274.8 12.5 %collective-permute-start.1 = (f32[4,128,128]{2,1,0:T(8,128)S(1)}, f32[4,128,128]{2,1,0:T(8,128)S(1)}, u32[]{:S(2)}, u32[]{:S(2)}) collective-permute-start(f32[4,128,128]{2,1,0:T(8,128)S(1)} %copy.62), channel_id=1, source_target_pairs={{16,0},{32,16},{48,32},{64,48},{80,64},{96,80},{112,96},{128,112},... | collective-permute-start | bytes 786440 | tf_op jit(solution)/shard_map/while/body/eval_jaxpr/ppermute | solution.py:13
  291.5 10.1 %collective-permute-start.13 = (f32[1,4,128,128]{3,2,1,0:T(8,128)S(1)}, f32[1,4,128,128]{3,2,1,0:T(8,128)S(1)}, u32[]{:S(2)}, u32[]{:S(2)}) collective-permute-start(f32[1,4,128,128]{3,2,1,0:T(8,128)S(1)} %broadcast_select_fusion.4), channel_id=1, source_target_pairs={{2,0},{3,1},{4,2},{5,3},{6,4},{7,5},{8,6},{9,7},{10,8},{11,9},{12,... | collective-permute-start | bytes 786440 | tf_op jit(solution)/shard_map/ppermute | solution.py:13
  301.6 10.4 %collective-permute-start.14 = (f32[1,4,128,128]{3,2,1,0:T(8,128)S(1)}, f32[1,4,128,128]{3,2,1,0:T(8,128)S(1)}, u32[]{:S(2)}, u32[]{:S(2)}) collective-permute-start(f32[1,4,128,128]{3,2,1,0:T(8,128)S(1)} %broadcast_select_fusion.6), channel_id=1, source_target_pairs={{4,0},{5,1},{6,2},{7,3},{8,4},{9,5},{10,6},{11,7},{12,8},{13,9},{1... | collective-permute-start | bytes 786440 | tf_op jit(solution)/shard_map/ppermute | solution.py:13
  312.0 8.9 %collective-permute-start.15 = (f32[1,4,128,128]{3,2,1,0:T(8,128)S(1)}, f32[1,4,128,128]{3,2,1,0:T(8,128)S(1)}, u32[]{:S(2)}, u32[]{:S(2)}) collective-permute-start(f32[1,4,128,128]{3,2,1,0:T(8,128)S(1)} %broadcast_select_fusion.8), channel_id=1, source_target_pairs={{8,0},{9,1},{10,2},{11,3},{12,4},{13,5},{14,6},{15,7},{0,8},{1,9},... | collective-permute-start | bytes 786440 | tf_op jit(solution)/shard_map/ppermute | solution.py:13
  320.9 8.4 %collective-permute-start.2 = (f32[4,128,128]{2,1,0:T(8,128)S(1)}, f32[4,128,128]{2,1,0:T(8,128)S(1)}, u32[]{:S(2)}, u32[]{:S(2)}) collective-permute-start(f32[4,128,128]{2,1,0:T(8,128)S(1)} %bitcast.169), channel_id=1, source_target_pairs={{1,0},{2,1},{3,2},{4,3},{5,4},{6,5},{7,6},{8,7},{9,8},{10,9},{11,1... | collective-permute-start | bytes 786440 | tf_op jit(solution)/shard_map/while/body/eval_jaxpr/ppermute | solution.py:13
  321.0 11.0 %collective-permute-start.3 = (f32[4,128,128]{2,1,0:T(8,128)S(1)}, f32[4,128,128]{2,1,0:T(8,128)S(1)}, u32[]{:S(2)}, u32[]{:S(2)}) collective-permute-start(f32[4,128,128]{2,1,0:T(8,128)S(1)} %copy.74), channel_id=1, source_target_pairs={{16,0},{32,16},{48,32},{64,48},{80,64},{96,80},{112,96},{128,112},... | collective-permute-start | bytes 786440 | tf_op jit(solution)/shard_map/while/body/eval_jaxpr/ppermute | solution.py:13
  332.1 8.8 %collective-permute-start.2 = (f32[4,128,128]{2,1,0:T(8,128)S(1)}, f32[4,128,128]{2,1,0:T(8,128)S(1)}, u32[]{:S(2)}, u32[]{:S(2)}) collective-permute-start(f32[4,128,128]{2,1,0:T(8,128)S(1)} %bitcast.169), channel_id=1, source_target_pairs={{1,0},{2,1},{3,2},{4,3},{5,4},{6,5},{7,6},{8,7},{9,8},{10,9},{11,1... | collective-permute-start | bytes 786440 | tf_op jit(solution)/shard_map/while/body/eval_jaxpr/ppermute | solution.py:13
  332.2 11.3 %collective-permute-start.3 = (f32[4,128,128]{2,1,0:T(8,128)S(1)}, f32[4,128,128]{2,1,0:T(8,128)S(1)}, u32[]{:S(2)}, u32[]{:S(2)}) collective-permute-start(f32[4,128,128]{2,1,0:T(8,128)S(1)} %copy.74), channel_id=1, source_target_pairs={{16,0},{32,16},{48,32},{64,48},{80,64},{96,80},{112,96},{128,112},... | collective-permute-start | bytes 786440 | tf_op jit(solution)/shard_map/while/body/eval_jaxpr/ppermute | solution.py:13
  343.5 8.3 %collective-permute-start.2 = (f32[4,128,128]{2,1,0:T(8,128)S(1)}, f32[4,128,128]{2,1,0:T(8,128)S(1)}, u32[]{:S(2)}, u32[]{:S(2)}) collective-permute-start(f32[4,128,128]{2,1,0:T(8,128)S(1)} %bitcast.169), channel_id=1, source_target_pairs={{1,0},{2,1},{3,2},{4,3},{5,4},{6,5},{7,6},{8,7},{9,8},{10,9},{11,1... | collective-permute-start | bytes 786440 | tf_op jit(solution)/shard_map/while/body/eval_jaxpr/ppermute | solution.py:13
  343.7 11.5 %collective-permute-start.3 = (f32[4,128,128]{2,1,0:T(8,128)S(1)}, f32[4,128,128]{2,1,0:T(8,128)S(1)}, u32[]{:S(2)}, u32[]{:S(2)}) collective-permute-start(f32[4,128,128]{2,1,0:T(8,128)S(1)} %copy.74), channel_id=1, source_target_pairs={{16,0},{32,16},{48,32},{64,48},{80,64},{96,80},{112,96},{128,112},... | collective-permute-start | bytes 786440 | tf_op jit(solution)/shard_map/while/body/eval_jaxpr/ppermute | solution.py:13
  355.2 9.5 %collective-permute-start.2 = (f32[4,128,128]{2,1,0:T(8,128)S(1)}, f32[4,128,128]{2,1,0:T(8,128)S(1)}, u32[]{:S(2)}, u32[]{:S(2)}) collective-permute-start(f32[4,128,128]{2,1,0:T(8,128)S(1)} %bitcast.169), channel_id=1, source_target_pairs={{1,0},{2,1},{3,2},{4,3},{5,4},{6,5},{7,6},{8,7},{9,8},{10,9},{11,1... | collective-permute-start | bytes 786440 | tf_op jit(solution)/shard_map/while/body/eval_jaxpr/ppermute | solution.py:13
  355.3 14.3 %collective-permute-start.3 = (f32[4,128,128]{2,1,0:T(8,128)S(1)}, f32[4,128,128]{2,1,0:T(8,128)S(1)}, u32[]{:S(2)}, u32[]{:S(2)}) collective-permute-start(f32[4,128,128]{2,1,0:T(8,128)S(1)} %copy.74), channel_id=1, source_target_pairs={{16,0},{32,16},{48,32},{64,48},{80,64},{96,80},{112,96},{128,112},... | collective-permute-start | bytes 786440 | tf_op jit(solution)/shard_map/while/body/eval_jaxpr/ppermute | solution.py:13
  369.6 9.2 %collective-permute-start.2 = (f32[4,128,128]{2,1,0:T(8,128)S(1)}, f32[4,128,128]{2,1,0:T(8,128)S(1)}, u32[]{:S(2)}, u32[]{:S(2)}) collective-permute-start(f32[4,128,128]{2,1,0:T(8,128)S(1)} %bitcast.169), channel_id=1, source_target_pairs={{1,0},{2,1},{3,2},{4,3},{5,4},{6,5},{7,6},{8,7},{9,8},{10,9},{11,1... | collective-permute-start | bytes 786440 | tf_op jit(solution)/shard_map/while/body/eval_jaxpr/ppermute | solution.py:13
  369.7 14.7 %collective-permute-start.3 = (f32[4,128,128]{2,1,0:T(8,128)S(1)}, f32[4,128,128]{2,1,0:T(8,128)S(1)}, u32[]{:S(2)}, u32[]{:S(2)}) collective-permute-start(f32[4,128,128]{2,1,0:T(8,128)S(1)} %copy.74), channel_id=1, source_target_pairs={{16,0},{32,16},{48,32},{64,48},{80,64},{96,80},{112,96},{128,112},... | collective-permute-start | bytes 786440 | tf_op jit(solution)/shard_map/while/body/eval_jaxpr/ppermute | solution.py:13
  384.4 8.2 %collective-permute-start.2 = (f32[4,128,128]{2,1,0:T(8,128)S(1)}, f32[4,128,128]{2,1,0:T(8,128)S(1)}, u32[]{:S(2)}, u32[]{:S(2)}) collective-permute-start(f32[4,128,128]{2,1,0:T(8,128)S(1)} %bitcast.169), channel_id=1, source_target_pairs={{1,0},{2,1},{3,2},{4,3},{5,4},{6,5},{7,6},{8,7},{9,8},{10,9},{11,1... | collective-permute-start | bytes 786440 | tf_op jit(solution)/shard_map/while/body/eval_jaxpr/ppermute | solution.py:13
  384.5 13.4 %collective-permute-start.3 = (f32[4,128,128]{2,1,0:T(8,128)S(1)}, f32[4,128,128]{2,1,0:T(8,128)S(1)}, u32[]{:S(2)}, u32[]{:S(2)}) collective-permute-start(f32[4,128,128]{2,1,0:T(8,128)S(1)} %copy.74), channel_id=1, source_target_pairs={{16,0},{32,16},{48,32},{64,48},{80,64},{96,80},{112,96},{128,112},... | collective-permute-start | bytes 786440 | tf_op jit(solution)/shard_map/while/body/eval_jaxpr/ppermute | solution.py:13
  398.0 7.9 %collective-permute-start.2 = (f32[4,128,128]{2,1,0:T(8,128)S(1)}, f32[4,128,128]{2,1,0:T(8,128)S(1)}, u32[]{:S(2)}, u32[]{:S(2)}) collective-permute-start(f32[4,128,128]{2,1,0:T(8,128)S(1)} %bitcast.169), channel_id=1, source_target_pairs={{1,0},{2,1},{3,2},{4,3},{5,4},{6,5},{7,6},{8,7},{9,8},{10,9},{11,1... | collective-permute-start | bytes 786440 | tf_op jit(solution)/shard_map/while/body/eval_jaxpr/ppermute | solution.py:13
  398.1 11.6 %collective-permute-start.3 = (f32[4,128,128]{2,1,0:T(8,128)S(1)}, f32[4,128,128]{2,1,0:T(8,128)S(1)}, u32[]{:S(2)}, u32[]{:S(2)}) collective-permute-start(f32[4,128,128]{2,1,0:T(8,128)S(1)} %copy.74), channel_id=1, source_target_pairs={{16,0},{32,16},{48,32},{64,48},{80,64},{96,80},{112,96},{128,112},... | collective-permute-start | bytes 786440 | tf_op jit(solution)/shard_map/while/body/eval_jaxpr/ppermute | solution.py:13
  409.8 10.9 %collective-permute-start.3 = (f32[4,128,128]{2,1,0:T(8,128)S(1)}, f32[4,128,128]{2,1,0:T(8,128)S(1)}, u32[]{:S(2)}, u32[]{:S(2)}) collective-permute-start(f32[4,128,128]{2,1,0:T(8,128)S(1)} %copy.74), channel_id=1, source_target_pairs={{16,0},{32,16},{48,32},{64,48},{80,64},{96,80},{112,96},{128,112},... | collective-permute-start | bytes 786440 | tf_op jit(solution)/shard_map/while/body/eval_jaxpr/ppermute | solution.py:13
  420.9 13.2 %collective-permute-start.3 = (f32[4,128,128]{2,1,0:T(8,128)S(1)}, f32[4,128,128]{2,1,0:T(8,128)S(1)}, u32[]{:S(2)}, u32[]{:S(2)}) collective-permute-start(f32[4,128,128]{2,1,0:T(8,128)S(1)} %copy.74), channel_id=1, source_target_pairs={{16,0},{32,16},{48,32},{64,48},{80,64},{96,80},{112,96},{128,112},... | collective-permute-start | bytes 786440 | tf_op jit(solution)/shard_map/while/body/eval_jaxpr/ppermute | solution.py:13
  434.2 8.3 %collective-permute-start.2 = (f32[4,128,128]{2,1,0:T(8,128)S(1)}, f32[4,128,128]{2,1,0:T(8,128)S(1)}, u32[]{:S(2)}, u32[]{:S(2)}) collective-permute-start(f32[4,128,128]{2,1,0:T(8,128)S(1)} %bitcast.169), channel_id=1, source_target_pairs={{1,0},{2,1},{3,2},{4,3},{5,4},{6,5},{7,6},{8,7},{9,8},{10,9},{11,1... | collective-permute-start | bytes 786440 | tf_op jit(solution)/shard_map/while/body/eval_jaxpr/ppermute | solution.py:13
  434.3 14.1 %collective-permute-start.3 = (f32[4,128,128]{2,1,0:T(8,128)S(1)}, f32[4,128,128]{2,1,0:T(8,128)S(1)}, u32[]{:S(2)}, u32[]{:S(2)}) collective-permute-start(f32[4,128,128]{2,1,0:T(8,128)S(1)} %copy.74), channel_id=1, source_target_pairs={{16,0},{32,16},{48,32},{64,48},{80,64},{96,80},{112,96},{128,112},... | collective-permute-start | bytes 786440 | tf_op jit(solution)/shard_map/while/body/eval_jaxpr/ppermute | solution.py:13
  448.5 12.7 %collective-permute-start.3 = (f32[4,128,128]{2,1,0:T(8,128)S(1)}, f32[4,128,128]{2,1,0:T(8,128)S(1)}, u32[]{:S(2)}, u32[]{:S(2)}) collective-permute-start(f32[4,128,128]{2,1,0:T(8,128)S(1)} %copy.74), channel_id=1, source_target_pairs={{16,0},{32,16},{48,32},{64,48},{80,64},{96,80},{112,96},{128,112},... | collective-permute-start | bytes 786440 | tf_op jit(solution)/shard_map/while/body/eval_jaxpr/ppermute | solution.py:13
  461.2 7.9 %collective-permute-start.2 = (f32[4,128,128]{2,1,0:T(8,128)S(1)}, f32[4,128,128]{2,1,0:T(8,128)S(1)}, u32[]{:S(2)}, u32[]{:S(2)}) collective-permute-start(f32[4,128,128]{2,1,0:T(8,128)S(1)} %bitcast.169), channel_id=1, source_target_pairs={{1,0},{2,1},{3,2},{4,3},{5,4},{6,5},{7,6},{8,7},{9,8},{10,9},{11,1... | collective-permute-start | bytes 786440 | tf_op jit(solution)/shard_map/while/body/eval_jaxpr/ppermute | solution.py:13
  461.4 11.2 %collective-permute-start.3 = (f32[4,128,128]{2,1,0:T(8,128)S(1)}, f32[4,128,128]{2,1,0:T(8,128)S(1)}, u32[]{:S(2)}, u32[]{:S(2)}) collective-permute-start(f32[4,128,128]{2,1,0:T(8,128)S(1)} %copy.74), channel_id=1, source_target_pairs={{16,0},{32,16},{48,32},{64,48},{80,64},{96,80},{112,96},{128,112},... | collective-permute-start | bytes 786440 | tf_op jit(solution)/shard_map/while/body/eval_jaxpr/ppermute | solution.py:13
  472.6 12.8 %collective-permute-start.3 = (f32[4,128,128]{2,1,0:T(8,128)S(1)}, f32[4,128,128]{2,1,0:T(8,128)S(1)}, u32[]{:S(2)}, u32[]{:S(2)}) collective-permute-start(f32[4,128,128]{2,1,0:T(8,128)S(1)} %copy.74), channel_id=1, source_target_pairs={{16,0},{32,16},{48,32},{64,48},{80,64},{96,80},{112,96},{128,112},... | collective-permute-start | bytes 786440 | tf_op jit(solution)/shard_map/while/body/eval_jaxpr/ppermute | solution.py:13
  485.5 7.9 %collective-permute-start.2 = (f32[4,128,128]{2,1,0:T(8,128)S(1)}, f32[4,128,128]{2,1,0:T(8,128)S(1)}, u32[]{:S(2)}, u32[]{:S(2)}) collective-permute-start(f32[4,128,128]{2,1,0:T(8,128)S(1)} %bitcast.169), channel_id=1, source_target_pairs={{1,0},{2,1},{3,2},{4,3},{5,4},{6,5},{7,6},{8,7},{9,8},{10,9},{11,1... | collective-permute-start | bytes 786440 | tf_op jit(solution)/shard_map/while/body/eval_jaxpr/ppermute | solution.py:13
  485.6 13.7 %collective-permute-start.3 = (f32[4,128,128]{2,1,0:T(8,128)S(1)}, f32[4,128,128]{2,1,0:T(8,128)S(1)}, u32[]{:S(2)}, u32[]{:S(2)}) collective-permute-start(f32[4,128,128]{2,1,0:T(8,128)S(1)} %copy.74), channel_id=1, source_target_pairs={{16,0},{32,16},{48,32},{64,48},{80,64},{96,80},{112,96},{128,112},... | collective-permute-start | bytes 786440 | tf_op jit(solution)/shard_map/while/body/eval_jaxpr/ppermute | solution.py:13
  499.4 7.9 %collective-permute-start.2 = (f32[4,128,128]{2,1,0:T(8,128)S(1)}, f32[4,128,128]{2,1,0:T(8,128)S(1)}, u32[]{:S(2)}, u32[]{:S(2)}) collective-permute-start(f32[4,128,128]{2,1,0:T(8,128)S(1)} %bitcast.169), channel_id=1, source_target_pairs={{1,0},{2,1},{3,2},{4,3},{5,4},{6,5},{7,6},{8,7},{9,8},{10,9},{11,1... | collective-permute-start | bytes 786440 | tf_op jit(solution)/shard_map/while/body/eval_jaxpr/ppermute | solution.py:13
  499.5 12.7 %collective-permute-start.3 = (f32[4,128,128]{2,1,0:T(8,128)S(1)}, f32[4,128,128]{2,1,0:T(8,128)S(1)}, u32[]{:S(2)}, u32[]{:S(2)}) collective-permute-start(f32[4,128,128]{2,1,0:T(8,128)S(1)} %copy.74), channel_id=1, source_target_pairs={{16,0},{32,16},{48,32},{64,48},{80,64},{96,80},{112,96},{128,112},... | collective-permute-start | bytes 786440 | tf_op jit(solution)/shard_map/while/body/eval_jaxpr/ppermute | solution.py:13
  512.2 7.9 %collective-permute-start.2 = (f32[4,128,128]{2,1,0:T(8,128)S(1)}, f32[4,128,128]{2,1,0:T(8,128)S(1)}, u32[]{:S(2)}, u32[]{:S(2)}) collective-permute-start(f32[4,128,128]{2,1,0:T(8,128)S(1)} %bitcast.169), channel_id=1, source_target_pairs={{1,0},{2,1},{3,2},{4,3},{5,4},{6,5},{7,6},{8,7},{9,8},{10,9},{11,1... | collective-permute-start | bytes 786440 | tf_op jit(solution)/shard_map/while/body/eval_jaxpr/ppermute | solution.py:13
  512.3 11.3 %collective-permute-start.3 = (f32[4,128,128]{2,1,0:T(8,128)S(1)}, f32[4,128,128]{2,1,0:T(8,128)S(1)}, u32[]{:S(2)}, u32[]{:S(2)}) collective-permute-start(f32[4,128,128]{2,1,0:T(8,128)S(1)} %copy.74), channel_id=1, source_target_pairs={{16,0},{32,16},{48,32},{64,48},{80,64},{96,80},{112,96},{128,112},... | collective-permute-start | bytes 786440 | tf_op jit(solution)/shard_map/while/body/eval_jaxpr/ppermute | solution.py:13
  (16 other events, 120.4 us)
